TPU v7x, 128 devices: a whole 4x4x4 slice. The times are simulated.
128 devices in a mesh: batch: 8 (over x, core), item: 16 (over y, z).
Axes of the slice: x: 4, y: 4, z: 4, core: 2. Of those that a mesh axis runs over, the one named last changes fastest.
Arguments:
- item_table: bfloat16 [32768, 256], P('item'), may hold values from -6 to 6
- neighbours: int32 [256, 32], P('item', 'batch'), may hold values from 0 to 255, as said below
- tile_weights: bfloat16 [256, 32, 128, 128], P('item', 'batch'), may hold values from -0.09375 to 0.09375
- history: int32 [2048, 256], P(('batch', 'item')), may hold values from 0 to 32767, as said below
- lengths: int32 [2048], P(('batch', 'item')), may hold values from 1 to 256, 262144 in all
- position: float32 [256, 256], replicated, may hold values from -3 to 3
- norm_gain: float32 [256], replicated, may hold values from 0.1 to 1.9
- in_weight: bfloat16 [256, 768], replicated, may hold values from -2 to 2
- out_weight: bfloat16 [256, 256], replicated, may hold values from -0.375 to 0.375
- cotangent: bfloat16 [2048, 256, 256], P(('batch', 'item')), may hold values from -0.032958984 to 0.032958984
Outputs:
- block_out: bfloat16 [2048, 256, 256], P(('batch', 'item'))
- grad_in_weight: float32 [256, 768], replicated
- grad_out_weight: float32 [256, 256], replicated
- grad_norm_gain: float32 [256], replicated
- grad_position: float32 [256, 256], replicated
Inputs may be any that keep to these rules, and one draw needn't show every extreme that they name: `neighbours`: row tile t lies on item shard s = t // 16; its slots name only tiles of shards s - 1, s and s + 1, taken cyclically over the shards; a tile may repeat among the slots. `history`: item ids fall into runs of 256 consecutive ids, run r holding ids r * 256 to (r + 1) * 256 - 1. The 4096 ids of each aligned block of 16 users (all positions, live or not) name every run exactly 32 times.
All inputs are finite; a program needn't handle non-finite values. No bound on the sum of `lengths` on one device may be relied on, other than what follows from the above.
Results may differ from a plain program's by a relative error of at most 0.029.
The roundings to bfloat16 on the way count: a program that leaves them out, or rounds other values in their place, can miss the bound.
Values may be sent and summed in bfloat16 or wider, within the bound.
No kernel may reach another device: no remote copies, remote signals or barrier semaphores. Data moves between devices by JAX's collectives and lax.ppermute only.
A program may use at most 64 MiB of HBM per device.

v0:
```python
import jax
import jax.numpy as jnp
from jax import lax
from jax.sharding import PartitionSpec as P

HEADS = 8


def padded(cells, sides, width):
    for axis, dim in sides:
        count = lax.axis_size(axis)
        head = lax.slice_in_dim(cells, 0, width, axis=dim)
        tail = lax.slice_in_dim(cells, cells.shape[dim] - width, cells.shape[dim], axis=dim)
        cells = jnp.concatenate(
            [
                lax.ppermute(tail, axis, [(i, (i + 1) % count) for i in range(count)]),
                cells,
                lax.ppermute(head, axis, [((i + 1) % count, i) for i in range(count)]),
            ],
            axis=dim,
        )
    return cells


def block_pass(rows_in, lens, cot_rows, position, norm_gain, in_weight, out_weight):
    group_size, length, feat_width = rows_in.shape
    head_dim = feat_width // HEADS
    score_scale = head_dim ** (-0.5)
    flat_count = group_size * length
    residual = rows_in.astype(jnp.float32) + position
    inv_rms = lax.rsqrt(jnp.mean(residual * residual, axis=-1, keepdims=True) + 1e-05)
    normed = (residual * inv_rms * norm_gain).astype(jnp.bfloat16)
    flat_normed = normed.reshape(flat_count, feat_width)
    qkv = jnp.dot(flat_normed, in_weight, preferred_element_type=jnp.float32).astype(jnp.bfloat16)
    query_rows = qkv[:, :feat_width].reshape(group_size, length, HEADS, head_dim)
    key_rows = qkv[:, feat_width : 2 * feat_width].reshape(group_size, length, HEADS, head_dim)
    value_rows = qkv[:, 2 * feat_width :].reshape(group_size, length, HEADS, head_dim)
    scores = (
        jnp.einsum("gihe,gjhe->ghij", query_rows, key_rows, preferred_element_type=jnp.float32)
        * score_scale
    )
    places = jnp.arange(length)
    allowed = (places[None, :] <= places[:, None])[None, None] & (
        places[None, None, None, :] < lens[:, None, None, None]
    )
    scores = jnp.where(allowed, scores, -1e30)
    row_top = jnp.max(scores, axis=-1, keepdims=True)
    weights_exp = jnp.where(allowed, jnp.exp(scores - row_top), 0.0)
    prob_full = weights_exp / jnp.sum(weights_exp, axis=-1, keepdims=True)
    probs_low = prob_full.astype(jnp.bfloat16)
    mixed_rows = jnp.einsum(
        "ghij,gjhe->gihe", probs_low, value_rows, preferred_element_type=jnp.float32
    )
    mixed_rows = mixed_rows.astype(jnp.bfloat16).reshape(flat_count, feat_width)
    attn_rows = jnp.dot(mixed_rows, out_weight, preferred_element_type=jnp.float32)
    live_mask = (places[None, :] < lens[:, None]).astype(jnp.float32).reshape(flat_count, 1)
    flat_resid = residual.reshape(flat_count, feat_width)
    block_rows = (
        (live_mask * (flat_resid + attn_rows))
        .astype(jnp.bfloat16)
        .reshape(group_size, length, feat_width)
    )
    grad_res = live_mask * cot_rows.reshape(flat_count, feat_width).astype(jnp.float32)
    grad_low = grad_res.astype(jnp.bfloat16)
    grad_out = jnp.dot(mixed_rows.T, grad_low, preferred_element_type=jnp.float32)
    grad_mixed = jnp.dot(grad_low, out_weight.T, preferred_element_type=jnp.float32).astype(
        jnp.bfloat16
    )
    grad_mixed = grad_mixed.reshape(group_size, length, HEADS, head_dim)
    grad_probs = jnp.einsum(
        "gihe,gjhe->ghij", grad_mixed, value_rows, preferred_element_type=jnp.float32
    )
    inner_sum = jnp.sum(prob_full * grad_probs, axis=-1, keepdims=True)
    grad_scores = (prob_full * (grad_probs - inner_sum) * score_scale).astype(jnp.bfloat16)
    grad_query = jnp.einsum(
        "ghij,gjhe->gihe", grad_scores, key_rows, preferred_element_type=jnp.float32
    ).astype(jnp.bfloat16)
    grad_key = jnp.einsum(
        "ghij,gihe->gjhe", grad_scores, query_rows, preferred_element_type=jnp.float32
    ).astype(jnp.bfloat16)
    grad_value = jnp.einsum(
        "ghij,gihe->gjhe", probs_low, grad_mixed, preferred_element_type=jnp.float32
    ).astype(jnp.bfloat16)
    grad_qkv = jnp.concatenate(
        [
            grad_query.reshape(flat_count, feat_width),
            grad_key.reshape(flat_count, feat_width),
            grad_value.reshape(flat_count, feat_width),
        ],
        axis=1,
    )
    grad_in = jnp.dot(flat_normed.T, grad_qkv, preferred_element_type=jnp.float32)
    grad_normed = jnp.dot(grad_qkv, in_weight.T, preferred_element_type=jnp.float32)
    flat_inv = inv_rms.reshape(flat_count, 1)
    scaled = grad_normed * norm_gain
    grad_gain = jnp.sum(grad_normed * flat_resid * flat_inv, axis=0)
    grad_resid = (
        grad_res
        + flat_inv * scaled
        - flat_resid
        * (flat_inv * flat_inv * flat_inv)
        * jnp.mean(scaled * flat_resid, axis=-1, keepdims=True)
    )
    grad_pos = jnp.sum(grad_resid.reshape(group_size, length, feat_width), axis=0)
    return (block_rows, (grad_in, grad_out, grad_gain, grad_pos))


def local(
    item_table,
    neighbours,
    tile_weights,
    history,
    lengths,
    position,
    norm_gain,
    in_weight,
    out_weight,
    cotangent,
):
    n_batch = lax.axis_size("batch")
    n_item = lax.axis_size("item")
    rows_item, feat_width = item_table.shape
    tile_size = tile_weights.shape[2]
    tiles_here = rows_item // tile_size
    rows_own = rows_item // n_batch
    all_tiles = n_item * tiles_here
    widened = padded(item_table, (("item", 0),), rows_item)
    rim_tiles = widened.reshape(3 * tiles_here, tile_size, feat_width)
    local_ids = jnp.mod(neighbours - (lax.axis_index("item") - 1) * tiles_here, all_tiles)
    picked = rim_tiles[local_ids]
    term_rows = jnp.einsum(
        "nkab,nkbd->nad", tile_weights, picked, preferred_element_type=jnp.float32
    )
    summed = lax.psum_scatter(
        term_rows.reshape(rows_own * lax.axis_size("batch"), feat_width),
        "batch",
        scatter_dimension=0,
        tiled=True,
    )
    own_rows = lax.dynamic_slice_in_dim(item_table, lax.axis_index("batch") * rows_own, rows_own, 0)
    propagated = (0.5 * (own_rows.astype(jnp.float32) + summed)).astype(jnp.bfloat16)
    users_here, length = history.shape
    tokens_here = users_here * length
    peer_count = n_batch * n_item
    per_peer = tokens_here // peer_count
    flat_ids = history.reshape(tokens_here)
    run_index = flat_ids // rows_own
    owner = jnp.mod(run_index, n_batch) * n_item + run_index // n_batch
    send_order = jnp.argsort(owner, stable=True)
    sent_ids = flat_ids[send_order].reshape(peer_count, per_peer)
    found = propagated[
        jnp.mod(
            lax.all_to_all(sent_ids, ("batch", "item"), split_axis=0, concat_axis=0, tiled=True),
            rows_own,
        )
    ]
    returned = lax.all_to_all(found, ("batch", "item"), split_axis=0, concat_axis=0, tiled=True)
    flat_rows = returned.reshape(tokens_here, feat_width)
    inverse = (
        jnp.zeros((tokens_here,), jnp.int32)
        .at[send_order]
        .set(jnp.arange(tokens_here, dtype=jnp.int32))
    )
    rows_in = flat_rows[inverse].reshape(users_here, length, feat_width)
    pair_size = 2
    pair_count = users_here // pair_size

    def scan_step(totals, scan_args):
        rows_pair, lens_pair, cot_pair = scan_args
        block_rows, grads = block_pass(
            rows_pair, lens_pair, cot_pair, position, norm_gain, in_weight, out_weight
        )
        new_totals = tuple((total + grad for total, grad in zip(totals, grads)))
        return (new_totals, block_rows)

    start_totals = (
        jnp.zeros((feat_width, 3 * feat_width), jnp.float32),
        jnp.zeros((feat_width, feat_width), jnp.float32),
        jnp.zeros((feat_width,), jnp.float32),
        jnp.zeros((length, feat_width), jnp.float32),
    )
    scan_inputs = (
        rows_in.reshape(pair_count, pair_size, length, feat_width),
        lengths.reshape(pair_count, pair_size),
        cotangent.reshape(pair_count, pair_size, length, feat_width),
    )
    totals, block_pieces = lax.scan(scan_step, start_totals, scan_inputs)
    block_out = block_pieces.reshape(users_here, length, feat_width)
    grad_in, grad_out, grad_gain, grad_pos = lax.psum(
        (totals[0], totals[1], totals[2], totals[3]), ("batch", "item")
    )
    return (block_out, grad_in, grad_out, grad_gain, grad_pos)


def solution(mesh):
    in_specs = (
        P("item", None),
        P("item", "batch"),
        P("item", "batch", None, None),
        P(("batch", "item"), None),
        P(("batch", "item")),
        P(),
        P(),
        P(),
        P(),
        P(("batch", "item"), None, None),
    )
    out_specs = (P(("batch", "item"), None, None), P(), P(), P(), P())
    return jax.shard_map(local, mesh=mesh, in_specs=in_specs, out_specs=out_specs, check_vma=False)
```

profile of v0, /device:TPU:1, one launch (start us, length us, event | category | flops | bytes accessed | tf_op | source)
XLA Modules:
  0.0 849.8 jit_solution(16953517091819530897)
XLA Ops:
  9.8 4.7 collective-permute-start.1
  15.3 22.1 %collective-permute-done = bf16[2048,256]{1,0:T(8,128)(2,1)S(1)} collective-permute-done((bf16[2048,256]{1,0:T(8,128)(2,1)}, bf16[2048,256]{1,0:T(8,128)(2,1)S(1)}, u32[]{:S(2)}, u32[]{:S(2)}) %collective-permute-start) | collective-permute-done | bytes 1048608 | tf_op jit(solution)/shard_map/ppermute | solution.py:16
  37.4 3.0 pad_maximum_fusion
  40.4 4.6 gather_fusion
  45.0 4.4 fusion.71
  49.5 5.8 sort.17
  55.3 23.0 %gather_fusion.1 = s32[4096]{0:T(1024)S(1)} fusion(s32[4096]{0:T(1024)S(1)} %bitcast.161, s32[4096]{0:T(1024)S(1)} %get-tuple-element.168), kind=kCustom, calls=%fused_computation.1 | custom fusion | bytes 49152 | tf_op jit(solution)/shard_map/gather | solution.py:150
  79.0 9.8 %all-to-all-start = ((s32[128,1,32]{2,1,0:T(1,128)}), s32[128,1,32]{2,1,0:T(1,128)S(1)}, u32[]{:S(2)}, u32[]{:S(2)}) async-start(s32[128,1,32]{2,1,0:T(1,128)} %bitcast.6), calls=%async_computation.1 | async-start | bytes 131072 | tf_op jit(solution)/shard_map/all_to_all | solution.py:153
  88.8 9.5 %all-to-all-done = s32[128,1,32]{2,1,0:T(1,128)S(1)} async-done(((s32[128,1,32]{2,1,0:T(1,128)}), s32[128,1,32]{2,1,0:T(1,128)S(1)}, u32[]{:S(2)}, u32[]{:S(2)}) %all-to-all-start) | async-done | bytes 16416 | tf_op jit(solution)/shard_map/all_to_all | solution.py:153
  99.5 16.9 %gather_fusion.2 = bf16[4096,256]{1,0:T(8,128)(2,1)} fusion(bf16[256,256]{1,0:T(8,128)(2,1)S(1)} %multiply_convert_fusion.5, s32[4096]{0:T(1024)S(1)} %broadcast_clamp_fusion), kind=kCustom, calls=%fused_computation.2 | custom fusion | bytes 4210688 | tf_op jit(solution)/shard_map/gather | solution.py:151
  116.5 5.6 all-to-all-start.1
  122.9 15.7 %scatter_custom_fusion = s32[4096]{0:T(1024)S(1)} fusion(s32[4096]{0:T(1024)S(1)} %get-tuple-element.167, s32[4096]{0:T(1024)S(1)} %iota.30, s32[]{:T(128)} %constant.100.clone.1), kind=kCustom, calls=%fused_computation.113 | custom fusion | bytes 16388 | tf_op jit(solution)/shard_map/scatter | solution.py:162
  138.6 12.8 %all-to-all-done.1 = bf16[128,32,256]{2,1,0:T(8,128)(2,1)} async-done(((bf16[128,32,256]{2,1,0:T(8,128)(2,1)}), bf16[128,32,256]{2,1,0:T(8,128)(2,1)}, u32[]{:S(2)}, u32[]{:S(2)}) %all-to-all-start.1) | async-done | bytes 2097184 | tf_op jit(solution)/shard_map/all_to_all | solution.py:157
  151.4 17.7 %gather_fusion.3 = bf16[4096,256]{1,0:T(8,128)(2,1)} fusion(bf16[4096,256]{1,0:T(8,128)(2,1)} %bitcast.9, s32[4096]{0:T(1024)S(1)} %fusion.60), kind=kCustom, calls=%fused_computation.3 | custom fusion | bytes 4210688 | tf_op jit(solution)/shard_map/gather | solution.py:164
  169.1 522.8 %while.19 = (s32[]{:T(128)}, f32[256,768]{1,0:T(8,128)}, f32[256,256]{1,0:T(8,128)}, f32[256]{0:T(256)}, f32[256,256]{1,0:T(8,128)}, /*index=5*/bf16[8,2,256,256...) while((s32[]{:T(128)}, f32[256,768]{1,0:T(8,128)}, ...), condition=%wide.region_11.12_spmd.clone, body=%wide.region_3.11_spmd.clone.sunk | while | flops 1240739328 | bytes 77604632 | solution.py:187
  180.8 3.9 fusion.146
  188.1 2.6 fusion.150
  195.6 3.0 fusion.149
  199.7 2.7 fusion.144
  202.4 7.1 fusion.148
  210.5 7.2 fusion.147
  245.0 3.9 fusion.146
  252.3 2.6 fusion.150
  259.8 3.0 fusion.149
  263.9 2.7 fusion.144
  266.6 7.1 fusion.148
  274.8 7.2 fusion.147
  310.5 3.9 fusion.146
  317.8 2.6 fusion.150
  325.4 3.0 fusion.149
  329.4 2.7 fusion.144
  332.1 7.1 fusion.148
  340.3 7.2 fusion.147
  376.0 3.9 fusion.146
  383.4 2.6 fusion.150
  390.9 3.0 fusion.149
  394.9 2.7 fusion.144
  397.6 7.1 fusion.148
  405.8 7.2 fusion.147
  441.5 3.9 fusion.146
  448.9 2.6 fusion.150
  456.4 3.0 fusion.149
  460.4 2.7 fusion.144
  463.1 7.1 fusion.148
  471.3 7.2 fusion.147
  507.0 3.9 fusion.146
  514.4 2.6 fusion.150
  521.9 3.0 fusion.149
  525.9 2.7 fusion.144
  528.7 7.1 fusion.148
  536.8 7.2 fusion.147
  572.5 3.9 fusion.146
  579.9 2.6 fusion.150
  587.4 3.0 fusion.149
  591.4 2.7 fusion.144
  594.2 7.1 fusion.148
  602.3 7.2 fusion.147
  638.0 3.9 fusion.146
  652.9 3.0 fusion.149
  657.0 2.7 fusion.144
  659.7 7.1 fusion.148
  667.8 7.2 fusion.147
  691.9 63.8 %psum.30 = f32[256]{0:T(256)} all-reduce(f32[256]{0:T(256)} %get-tuple-element.81), channel_id=1, replica_groups=mesh['batch'=8,'item'=16] {'batch','item'}, use_global_device_ids=true, to_apply=%region_14.15 | all-reduce | flops 256 | bytes 2048 | tf_op jit(solution)/shard_map/psum | solution.py:189
  755.7 81.9 %all-reduce.3.cloned.1.call-done = (f32[256,768]{1,0:T(8,128)}, f32[256,256]{1,0:T(8,128)}, f32[256,256]{1,0:T(8,128)}) async-done(((f32[256,768]{1,0:T(8,128)}, f32[256,256]{1,0:T(8,128)}, f32[256,256]{1,0:T(8,128)}), (f32[256,768]{1,0:T(8,128)}, f32[256,256]{1,0:T(8,128)}, f32[256,256]{1,0:T(8,128)})) %all-reduce.3.cloned.1.call-update) | async-done | bytes 1310736 | tf_op jit(solution)/shard_map/psum | solution.py:189
  (450 shorter events, 323.1 us)
Async XLA Ops:
  7.2 37.9 %copy-start = (bf16[16,4,128,128]{3,2,1,0:T(8,128)(2,1)S(1)}, bf16[16,4,128,128]{3,2,1,0:T(8,128)(2,1)}, u32[]{:S(2)}) copy-start(bf16[16,4,128,128]{3,2,1,0:T(8,128)(2,1)} %param.14) | copy-start | bytes 6291460
  7.2 91.3 %reduce-scatter.2.cloned.1.call-start = ((), (), s32[]{:S(2)}) async-start(), calls=%async_computation.3 | async-start | bytes 2359296 | tf_op jit(solution)/shard_map/reduce_scatter | solution.py:134
  7.2 30.2 %collective-permute-start = (bf16[2048,256]{1,0:T(8,128)(2,1)}, bf16[2048,256]{1,0:T(8,128)(2,1)S(1)}, u32[]{:S(2)}, u32[]{:S(2)}) collective-permute-start(bf16[2048,256]{1,0:T(8,128)(2,1)} %param.12), channel_id=1, source_target_pairs={{0,1},{1,2},{2,3},{3,4},{4,5},{5,6},{6,7},{7,8},{8,9},{9,10},{10,1... | collective-permute-start | bytes 3145736 | tf_op jit(solution)/shard_map/ppermute | solution.py:16
  9.8 27.7 %collective-permute-start.1 = (bf16[2048,256]{1,0:T(8,128)(2,1)}, bf16[2048,256]{1,0:T(8,128)(2,1)}, u32[]{:S(2)}, u32[]{:S(2)}) collective-permute-start(bf16[2048,256]{1,0:T(8,128)(2,1)} %param.12), channel_id=1, source_target_pairs={{1,0},{2,1},{3,2},{4,3},{5,4},{6,5},{7,6},{8,7},{9,8},{10,9},{11,1... | collective-permute-start | bytes 3145736 | tf_op jit(solution)/shard_map/ppermute | solution.py:18
  45.0 4.4 copy-start.6
  79.0 19.3 %all-to-all-start = ((s32[128,1,32]{2,1,0:T(1,128)}), s32[128,1,32]{2,1,0:T(1,128)S(1)}, u32[]{:S(2)}, u32[]{:S(2)}) async-start(s32[128,1,32]{2,1,0:T(1,128)} %bitcast.6), calls=%async_computation.1 | async-start | bytes 131072 | tf_op jit(solution)/shard_map/all_to_all | solution.py:153
  116.5 5.7 copy-start.7
  116.5 34.9 %all-to-all-start.1 = ((bf16[128,32,256]{2,1,0:T(8,128)(2,1)}), bf16[128,32,256]{2,1,0:T(8,128)(2,1)}, u32[]{:S(2)}, u32[]{:S(2)}) async-start(bf16[128,32,256]{2,1,0:T(8,128)(2,1)} %bitcast.178), calls=%async_computation.2 | async-start | bytes 4194304 | tf_op jit(solution)/shard_map/all_to_all | solution.py:157
  122.1 715.5 %all-reduce.3.cloned.1.call-start = ((), (), s32[]{:S(2)}) async-start(), calls=%async_computation.4 | async-start | bytes 2621440 | tf_op jit(solution)/shard_map/psum | solution.py:189
  151.4 17.7 %copy-start.4 = (bf16[256,256]{1,0:T(8,128)(2,1)S(1)}, bf16[256,256]{1,0:T(8,128)(2,1)}, u32[]{:S(2)}) copy-start(bf16[256,256]{1,0:T(8,128)(2,1)} %param.20) | copy-start | bytes 393220
  151.4 17.7 %copy-start.5 = (f32[256]{0:T(256)S(1)}, f32[256]{0:T(256)}, u32[]{:S(2)}) copy-start(f32[256]{0:T(256)} %param.18) | copy-start | bytes 3076
  191.1 0.7 copy-start.1
  195.6 4.0 copy-start.2
  195.6 4.0 copy-start.3
  255.3 0.7 copy-start.1
  259.8 4.0 copy-start.2
  259.8 4.0 copy-start.3
  320.8 0.7 copy-start.1
  325.3 4.0 copy-start.2
  325.3 4.0 copy-start.3
  386.3 0.7 copy-start.1
  390.9 4.0 copy-start.2
  390.9 4.0 copy-start.3
  451.8 0.7 copy-start.1
  456.4 4.0 copy-start.2
  456.4 4.0 copy-start.3
  517.3 0.7 copy-start.1
  521.9 4.0 copy-start.2
  521.9 4.0 copy-start.3
  582.9 0.7 copy-start.1
  587.4 4.0 copy-start.2
  587.4 4.0 copy-start.3
  648.4 0.7 copy-start.1
  652.9 4.0 copy-start.2
  652.9 4.0 copy-start.3
Sparse Core Ops, SparseCore 0:
  49.6 32.1 reduce-scatter.1
  692.0 145.4 all-reduce.2
where the time goes:
time: 855 us; the launch traced here: 850 us
  matrix products  264 us (31%)
  local copies, waits for them, and re-layouts  213 us (25%)
  other arithmetic  144 us (17%)
  waiting for transfers between devices  126 us (15%)
  blocking collectives  63.8 us (7%)
  starting transfers between devices  22.7 us (3%)
  between operations  14.2 us (2%)
    psum x1, waiting for transfers between devices, local(): lax.psum((totals[0], totals[1], totals[2], totals[3]), ('batch', 'item'))  81.9 us
    psum x1, blocking collectives, local(): lax.psum((totals[0], totals[1], totals[2], totals[3]), ('batch', 'item'))  63.8 us
    dot_general x8, matrix products, block_pass(): jnp.einsum('ghij,gjhe->gihe', grad_scores, key_rows, preferred_element_ty...  57.4 us
    dot_general x8, matrix products, block_pass(): jnp.einsum('ghij,gihe->gjhe', grad_scores, query_rows, preferred_element_...  57 us
    sub x8, other arithmetic, block_pass(): weights_exp = jnp.where(allowed, jnp.exp(scores - row_top), 0.0)  31.1 us
    while x112, local copies, waits for them, and re-layouts  26.1 us
    add x16, other arithmetic, scan_step(): new_totals = tuple((total + grad for total, grad in zip(totals, grads)))  24 us
    dot_general x8, matrix products, block_pass(): jnp.einsum('ghij,gihe->gjhe', probs_low, grad_mixed, preferred_element_ty...  23.9 us
  transfers between devices with their start and end apart: 6, of which 4 were waited for; matrix products, arithmetic and copies ran while one was open for 5% of the time, Pallas kernels for 0%

commit v1 on v0

v1 whole, which is shorter than its diff:
```python
import functools
import jax
import jax.numpy as jnp
from jax import lax
from jax.experimental import pallas as pl
from jax.experimental.pallas import tpu as pltpu
from jax.sharding import PartitionSpec as P

PART_TYPE = jnp.bfloat16
SPREAD_TYPE = jnp.bfloat16
HEADS = 8
BLK = 128
NT = (((1,), (1,)), ((), ()))
TN = (((0,), (0,)), ((), ()))


def dotf(a, b, dims=(((1,), (0,)), ((), ()))):
    return lax.dot_general(a, b, dims, preferred_element_type=jnp.float32)


def diag2(top, low):
    return jnp.concatenate(
        [
            jnp.concatenate([top, jnp.zeros_like(top)], axis=1),
            jnp.concatenate([jnp.zeros_like(low), low], axis=1),
        ],
        axis=0,
    )


def user_pass(
    n, live_len, x_ref, cot_ref, pos_ref, gain_ref, win_ref, wint_ref, wout_ref,
    blk_ref, gin_ref, gout_ref, ggain_ref, gpos_ref, gkt_ref, gvt_ref, mxt_ref, gqt_ref,
):
    feat = pos_ref.shape[1]
    hd = feat // HEADS
    scale = hd ** (-0.5)
    bf = jnp.bfloat16
    resid = x_ref[:n, :] + pos_ref[:n, :]
    inv = lax.rsqrt(jnp.mean(resid * resid, axis=1, keepdims=True) + 1e-05)
    gain = gain_ref[...]
    rnorm = resid * inv
    normed = (rnorm * gain).astype(bf)
    kv = dotf(normed, win_ref[:, feat:]).astype(bf)
    qkvt = dotf(wint_ref[...], normed, NT).astype(bf)
    live = lax.broadcasted_iota(jnp.int32, (n, feat), 0) < live_len
    gres = jnp.where(live, cot_ref[0, :n, :].astype(jnp.float32), 0.0)
    glow = gres.astype(bf)
    gmt = dotf(wout_ref[...], glow, NT).astype(bf)
    lane = lax.broadcasted_iota(jnp.int32, (BLK, 2 * BLK), 1)
    causal = lax.broadcasted_iota(jnp.int32, (BLK, 2 * BLK), 0) <= (lane & (BLK - 1))
    for pair in range(HEADS // 2):
        r0 = 2 * hd * pair
        quad = 128 * (r0 // 128)
        off = r0 - quad
        kq = kv[:, quad : quad + 128]
        vq = kv[:, feat + quad : feat + quad + 128]
        kt = qkvt[feat + r0 : feat + r0 + 2 * hd, :]
        vt = qkvt[2 * feat + r0 : 2 * feat + r0 + 2 * hd, :]
        for ib in range(n // BLK):
            i0 = ib * BLK
            nj = i0 + BLK
            qd = diag2(qkvt[r0 : r0 + hd, i0:nj], qkvt[r0 + hd : r0 + 2 * hd, i0:nj])
            md = diag2(gmt[r0 : r0 + hd, i0:nj], gmt[r0 + hd : r0 + 2 * hd, i0:nj])
            fill = jnp.zeros((2 * hd, 2 * BLK), bf)
            widen = lambda d: jnp.concatenate([d, fill] if off == 0 else [fill, d], axis=0)
            sc = dotf(kq[:nj], widen(qd)) * scale
            edge = jnp.where(causal, sc[i0:], -1e30)
            sc = edge if ib == 0 else jnp.concatenate([sc[:i0], edge], axis=0)
            top = jnp.max(sc, axis=0, keepdims=True)
            ex = jnp.exp(sc - top)
            prob = ex * (1.0 / jnp.sum(ex, axis=0, keepdims=True))
            plow = prob.astype(bf)
            mt = dotf(vt[:, :nj], plow)
            mxt_ref[r0 : r0 + hd, i0:nj] = mt[:hd, :BLK].astype(bf)
            mxt_ref[r0 + hd : r0 + 2 * hd, i0:nj] = mt[hd:, BLK:].astype(bf)
            gp = dotf(vq[:nj], widen(md))
            inner = jnp.sum(prob * gp, axis=0, keepdims=True)
            gs = (prob * (gp - inner) * scale).astype(bf)
            gq = dotf(kt[:, :nj], gs)
            gqt_ref[r0 : r0 + hd, i0:nj] = gq[:hd, :BLK].astype(bf)
            gqt_ref[r0 + hd : r0 + 2 * hd, i0:nj] = gq[hd:, BLK:].astype(bf)
            gk = dotf(qd, gs, NT)
            gv = dotf(md, plow, NT)
            if n > BLK and ib == 0:
                gkt_ref[r0 : r0 + 2 * hd, :] = gk
                gvt_ref[r0 : r0 + 2 * hd, :] = gv
            else:
                if ib > 0:
                    ones = [gkt_ref[r0 : r0 + 2 * hd, :], gvt_ref[r0 : r0 + 2 * hd, :]]
                    gk = jnp.concatenate([gk[:, :BLK] + ones[0], gk[:, BLK:]], axis=1)
                    gv = jnp.concatenate([gv[:, :BLK] + ones[1], gv[:, BLK:]], axis=1)
                gqt_ref[feat + r0 : feat + r0 + 2 * hd, :n] = gk.astype(bf)
                gqt_ref[2 * feat + r0 : 2 * feat + r0 + 2 * hd, :n] = gv.astype(bf)
    mxt = mxt_ref[:, :n]
    attn = dotf(mxt, wout_ref[...], TN)
    blk_ref[0, :n, :] = jnp.where(live, resid + attn, 0.0).astype(bf)
    if n < blk_ref.shape[1]:
        blk_ref[0, n:, :] = jnp.zeros((blk_ref.shape[1] - n, feat), bf)
    gout_ref[...] += dotf(mxt, glow)
    gqkvt = gqt_ref[:, :n]
    gin_ref[...] += dotf(gqkvt, normed)
    gn = dotf(win_ref[...], gqkvt).T
    scaled = gn * gain
    ggain_ref[...] += jnp.sum(gn * rnorm, axis=0, keepdims=True)
    corr = jnp.mean(scaled * resid, axis=1, keepdims=True) * (inv * inv * inv)
    gpos_ref[:n, :] += gres + inv * scaled - resid * corr


def attn_kernel(
    lens_ref, idx_ref, rows_ref, cot_ref, pos_ref, gain_ref, win_ref, wint_ref, wout_ref,
    blk_ref, pack_ref, rowf_ref, x_ref, gkt_ref, gvt_ref, mxt_ref, gqt_ref,
    gin_ref, gout_ref, ggain_ref, gpos_ref,
):
    u = pl.program_id(0)
    length = x_ref.shape[0]

    @pl.when(u == 0)
    def _():
        rowf_ref[...] = rows_ref[...].astype(jnp.float32)
        gin_ref[...] = jnp.zeros_like(gin_ref)
        gout_ref[...] = jnp.zeros_like(gout_ref)
        ggain_ref[...] = jnp.zeros_like(ggain_ref)
        gpos_ref[...] = jnp.zeros_like(gpos_ref)

    live_len = lens_ref[u]

    def run(n):
        def eight(g, carry):
            base = pl.multiple_of(g * 8, 8)
            for k in range(8):
                r = idx_ref[u * length + base + k]
                x_ref[pl.ds(base + k, 1), :] = rowf_ref[pl.ds(r, 1), :]
            return carry

        lax.fori_loop(0, n // 8, eight, 0)
        user_pass(
            n, live_len, x_ref, cot_ref, pos_ref, gain_ref, win_ref, wint_ref, wout_ref,
            blk_ref, gin_ref, gout_ref, ggain_ref, gpos_ref, gkt_ref, gvt_ref, mxt_ref, gqt_ref,
        )

    @pl.when(live_len <= BLK)
    def _():
        run(BLK)

    @pl.when(live_len > BLK)
    def _():
        run(length)

    @pl.when(u == pl.num_programs(0) - 1)
    def _():
        feat = gpos_ref.shape[1]
        gin = gin_ref[...].T
        at = 0
        for whole in (gin, gout_ref[...], gpos_ref[...]):
            for c in range(whole.shape[1] // 128):
                pack_ref[at : at + feat, :] = whole[:, 128 * c : 128 * c + 128].astype(pack_ref.dtype)
                at += feat
        tail = pack_ref.shape[0] - at
        pack_ref[at:, :] = jnp.zeros((tail, 128), pack_ref.dtype)
        row = lax.broadcasted_iota(jnp.int32, (16, 128), 0)
        gg = ggain_ref[...]
        both = jnp.where(row == 0, gg[:, :128], jnp.where(row == 1, gg[:, 128:], 0.0))
        pack_ref[at : at + 16, :] = both.astype(pack_ref.dtype)


def attention(rows, idx, lengths, cot, position, gain, win, wint, wout, pack_rows, pack_type):
    users, length, feat = cot.shape
    whole = lambda a: pl.BlockSpec(a.shape, lambda u, *_: (0,) * a.ndim, pipeline_mode=pl.Buffered(1))
    per_user = pl.BlockSpec((1, length, feat), lambda u, *_: (u, 0, 0))
    gain = gain.reshape(1, feat)
    f32, bf = jnp.float32, jnp.bfloat16
    return pl.pallas_call(
        attn_kernel,
        out_shape=(
            jax.ShapeDtypeStruct((users, length, feat), bf),
            jax.ShapeDtypeStruct((pack_rows, 128), pack_type),
        ),
        grid_spec=pltpu.PrefetchScalarGridSpec(
            num_scalar_prefetch=2,
            grid=(users,),
            in_specs=[whole(rows), per_user, whole(position), whole(gain), whole(win), whole(wint), whole(wout)],
            out_specs=[per_user, pl.BlockSpec((pack_rows, 128), lambda u, *_: (0, 0))],
            scratch_shapes=[
                pltpu.VMEM(rows.shape, f32),
                pltpu.VMEM((length, feat), f32),
                pltpu.VMEM((feat, BLK), f32),
                pltpu.VMEM((feat, BLK), f32),
                pltpu.VMEM((feat, length), bf),
                pltpu.VMEM((3 * feat, length), bf),
                pltpu.VMEM((3 * feat, feat), f32),
                pltpu.VMEM((feat, feat), f32),
                pltpu.VMEM((1, feat), f32),
                pltpu.VMEM((length, feat), f32),
            ],
        ),
        compiler_params=pltpu.CompilerParams(
            dimension_semantics=("arbitrary",), vmem_limit_bytes=48 * 2**20
        ),
    )(lengths, idx, rows, cot, position, gain, win, wint, wout)


def route_kernel(n_batch, n_item, hist_ref, sent_ref, place_ref):
    users, length = hist_ref.shape
    peers, per_peer = sent_ref.shape
    rows_own = 256
    f32, bf = jnp.float32, jnp.bfloat16
    peer_row = lax.broadcasted_iota(jnp.int32, (peers, length), 0)
    slot_row = lax.broadcasted_iota(jnp.int32, (per_peer, length), 0)
    before = (
        lax.broadcasted_iota(jnp.int32, (length, length), 0)
        < lax.broadcasted_iota(jnp.int32, (length, length), 1)
    ).astype(f32).astype(bf)
    counts = jnp.zeros((peers, 1), f32)
    sent = jnp.zeros((peers, per_peer), f32)
    for u in range(users):
        ids = hist_ref[u : u + 1, :]
        run = ids // rows_own
        owner = (run % n_batch) * n_item + run // n_batch
        inside = (ids % rows_own).astype(f32)
        mine = (peer_row == owner).astype(f32)
        ahead = dotf(mine.astype(bf), before) + counts
        rank = jnp.sum(mine * ahead, axis=0, keepdims=True)
        counts = counts + jnp.sum(mine, axis=1, keepdims=True)
        rank_int = rank.astype(jnp.int32)
        place_ref[u : u + 1, :] = owner * per_peer + rank_int
        slot = (slot_row == rank_int).astype(f32).astype(bf)
        sent = sent + dotf((mine * inside).astype(bf), slot, NT)
    sent_ref[...] = sent.astype(jnp.int32)


def route(history, n_batch, n_item):
    users, length = history.shape
    peers = n_batch * n_item
    per_peer = users * length // peers
    return pl.pallas_call(
        functools.partial(route_kernel, n_batch, n_item),
        out_shape=(
            jax.ShapeDtypeStruct((peers, per_peer), jnp.int32),
            jax.ShapeDtypeStruct((users, length), jnp.int32),
        ),
        name="route",
    )(history)


def graph_kernel(
    tile_ref, part_ref, left_ref, own_ref, right_ref, weights_ref, wanted_ref, found_ref, table, sems
):
    rows_item, feat = own_ref.shape
    tile = weights_ref.shape[-1]
    tiles_here = rows_item // tile
    copies = [
        pltpu.make_async_copy(src, table.at[pl.ds(i * rows_item, rows_item)], sems.at[i])
        for i, src in enumerate((left_ref, own_ref, right_ref))
    ]
    for c in copies:
        c.start()
    for c in copies:
        c.wait()
    groups, row_tiles, slots = weights_ref.shape[:3]

    def tile_of(g, n, k):
        place = tile_ref[(g * row_tiles + n) * slots + k]
        return table[pl.ds(pl.multiple_of(place * tile, tile), tile), :]

    halves = []
    for n in range(row_tiles):
        acc = jnp.zeros((tile, feat), jnp.float32)
        for g in range(groups):
            for k in range(0, slots, 2):
                lhs = jnp.concatenate([weights_ref[g, n, k], weights_ref[g, n, k + 1]], axis=1)
                rhs = jnp.concatenate([tile_of(g, n, k), tile_of(g, n, k + 1)], axis=0)
                acc = acc + dotf(lhs, rhs)
        start = pl.multiple_of(rows_item + (part_ref[0] * row_tiles + n) * tile, tile)
        own = table[pl.ds(start, tile), :].astype(jnp.float32)
        halves.append((0.5 * (own + acc)).astype(jnp.bfloat16))
    propagated = jnp.concatenate(halves, axis=0)
    columns = wanted_ref[...].astype(jnp.float32).T
    spot = lax.broadcasted_iota(jnp.int32, (128, row_tiles * tile), 1).astype(jnp.float32)
    for b in range(columns.shape[1]):
        pick = (columns[:, b : b + 1] == spot).astype(jnp.float32).astype(jnp.bfloat16)
        found_ref[128 * b : 128 * b + 128, :] = dotf(pick, propagated).astype(jnp.bfloat16)


def graph(tile_ids, part, left, own, right, weights, wanted):
    rows_item, feat = own.shape
    anywhere = pl.BlockSpec(memory_space=pl.ANY)
    whole = lambda a: pl.BlockSpec(a.shape, lambda i, *_: (0,) * a.ndim)
    count = wanted.shape[0] * wanted.shape[1]
    return pl.pallas_call(
        graph_kernel,
        out_shape=jax.ShapeDtypeStruct((count, feat), jnp.bfloat16),
        grid_spec=pltpu.PrefetchScalarGridSpec(
            num_scalar_prefetch=2,
            grid=(1,),
            in_specs=[anywhere, anywhere, anywhere, whole(weights), whole(wanted)],
            out_specs=pl.BlockSpec((count, feat), lambda i, *_: (0, 0)),
            scratch_shapes=[
                pltpu.VMEM((3 * rows_item, feat), jnp.bfloat16),
                pltpu.SemaphoreType.DMA((3,)),
            ],
        ),
        compiler_params=pltpu.CompilerParams(vmem_limit_bytes=40 * 2**20),
        name="graph",
    )(tile_ids, part, left, own, right, weights, wanted)


def sum_kernel(parts_ref, out_ref):
    total = jnp.sum(parts_ref[...].astype(jnp.float32), axis=0, keepdims=True)
    out_ref[...] = jnp.broadcast_to(total, out_ref.shape).astype(out_ref.dtype)


def sum_spread(parts, spread_type):
    return pl.pallas_call(
        sum_kernel,
        out_shape=jax.ShapeDtypeStruct(parts.shape, spread_type),
        compiler_params=pltpu.CompilerParams(vmem_limit_bytes=40 * 2**20),
        name="sum_spread",
    )(parts)


def exchange(cells, axes):
    return lax.all_to_all(cells, axes, split_axis=0, concat_axis=0, tiled=True)


def local(
    item_table, neighbours, tile_weights, history, lengths, position, norm_gain,
    in_weight, out_weight, cotangent,
):
    n_batch = lax.axis_size("batch")
    n_item = lax.axis_size("item")
    peers = n_batch * n_item
    everyone = ("batch", "item")
    rows_item, feat = item_table.shape
    tile = tile_weights.shape[2]
    tiles_here = rows_item // tile
    slots = tile_weights.shape[1]
    row_tiles = tiles_here // n_batch
    here = lax.axis_index("item")
    users_here, length = history.shape
    left = lax.ppermute(item_table, "item", [(i, (i + 1) % n_item) for i in range(n_item)])
    right = lax.ppermute(item_table, "item", [((i + 1) % n_item, i) for i in range(n_item)])
    weights = exchange(tile_weights, "batch").reshape(n_batch, row_tiles, slots, tile, tile)
    sent, place = route(history, n_batch, n_item)
    per_peer = sent.shape[1]
    rim = jnp.mod(neighbours - (here - 1) * tiles_here, n_item * tiles_here)
    rim = jnp.broadcast_to(
        rim.reshape(n_batch, 1, row_tiles * slots), (n_batch, n_item, row_tiles * slots)
    ).reshape(peers, row_tiles * slots)
    got = exchange(jnp.concatenate([sent, rim], axis=1), everyone)
    wanted = got[:, :per_peer].reshape(-1, 128)
    tile_ids = lax.dynamic_index_in_dim(
        got[:, per_peer:].reshape(n_batch, n_item, row_tiles * slots), here, 1, keepdims=False
    ).reshape(-1)
    part = lax.axis_index("batch").reshape(1)
    found = graph(tile_ids, part, left, item_table, right, weights, wanted)
    rows = exchange(found.reshape(peers, per_peer, feat), everyone).reshape(-1, feat)
    pack_rows = peers * 24
    block_out, packed = attention(
        rows, place.reshape(-1), lengths, cotangent, position, norm_gain, in_weight,
        in_weight.T, out_weight, pack_rows, PART_TYPE,
    )
    parts = exchange(packed.reshape(peers, pack_rows // peers, 128), everyone)
    full = exchange(sum_spread(parts, SPREAD_TYPE), everyone).reshape(pack_rows, 128)
    full = full.astype(jnp.float32)
    slab = lambda a, b: jnp.concatenate(
        [full[feat * i : feat * i + feat] for i in range(a, b)], axis=1
    )
    gain_row = 10 * feat
    return (
        block_out,
        slab(0, 6),
        slab(6, 8),
        full[gain_row : gain_row + 2].reshape(feat),
        slab(8, 10),
    )


def solution(mesh):
    in_specs = (
        P("item", None),
        P("item", "batch"),
        P("item", "batch", None, None),
        P(("batch", "item"), None),
        P(("batch", "item")),
        P(),
        P(),
        P(),
        P(),
        P(("batch", "item"), None, None),
    )
    out_specs = (P(("batch", "item"), None, None), P(), P(), P(), P())
    return jax.shard_map(local, mesh=mesh, in_specs=in_specs, out_specs=out_specs, check_vma=False)
```

time: 855 us -> 229 us (0.27)
  matrix products: 264 us -> 0 us
  local copies, waits for them, and re-layouts: 213 us -> 5.51 us
  other arithmetic: 144 us -> 1.8 us
  waiting for transfers between devices: 126 us -> 52.3 us
  Pallas kernels: 0 us -> 70.8 us
  blocking collectives: 63.8 us -> 79.5 us
  between operations: 14.2 us -> 0.82 us
    dot_general x97 -> x0, matrix products: 264 us -> none  [the longest x8 57.4 us: block_pass(): jnp.einsum('ghij,gjhe->gihe', grad_scores, key_rows, preferred_element_ty...]
    psum x1 -> x0, waiting for transfers between devices: 81.9 us -> none  [local(): lax.psum((totals[0], totals[1], totals[2], totals[3]), ('batch', 'item'))]
    all_to_all x0 -> x3, blocking collectives: none -> 79.5 us  [exchange(): return lax.all_to_all(cells, axes, split_axis=0, concat_axis=0, tiled=True)]
    pallas_call x0 -> x4, Pallas kernels: none -> 70.8 us  [the longest x1 64.3 us: attention(): pl.pallas_call(attn_kernel, out_shape=(jax.ShapeDtypeStruct((users, lengt...]
    psum x1 -> x0, blocking collectives: 63.8 us -> none  [local(): lax.psum((totals[0], totals[1], totals[2], totals[3]), ('batch', 'item'))]
    gather x4 -> x0, local copies, waits for them, and re-layouts: 62.3 us -> none  [the longest x1 23 us: local(): sent_ids = flat_ids[send_order].reshape(peer_count, per_peer)]
    sub x16 -> x0, other arithmetic: 47.7 us -> none  [the longest x8 31.1 us: block_pass(): weights_exp = jnp.where(allowed, jnp.exp(scores - row_top), 0.0)]
    slice x32 -> x2, local copies, waits for them, and re-layouts: 36.7 us -> 0.12 us  [the longest x1 0.08 us: local(): got[:, per_peer:].reshape(n_batch, n_item, row_tiles * slots)]
  transfers between devices with their start and end apart: 6 -> 4, of which waited for: 4 -> 2; matrix products, arithmetic and copies ran while one was open for 5% -> 0% of each run, Pallas kernels for 0% -> 0%
where the time goes in v1:
time: 229 us; the launch traced here: 230 us
  blocking collectives  79.5 us (35%)
  Pallas kernels  70.8 us (31%)
  waiting for transfers between devices  52.3 us (23%)
  starting transfers between devices  18.9 us (8%)
  local copies, waits for them, and re-layouts  5.51 us (2%)
    all_to_all x3, blocking collectives, exchange(): return lax.all_to_all(cells, axes, split_axis=0, concat_axis=0, tiled=True)  79.5 us
    pallas_call x1, Pallas kernels, attention(): pl.pallas_call(attn_kernel, out_shape=(jax.ShapeDtypeStruct((users, lengt...  64.3 us
    all_to_all x2, waiting for transfers between devices, exchange(): return lax.all_to_all(cells, axes, split_axis=0, concat_axis=0, tiled=True)  29.3 us
    ppermute x1, waiting for transfers between devices, local(): lax.ppermute(item_table, 'item', [(i, (i + 1) % n_item) for i in range(n_...  23 us
    all_to_all x2, starting transfers between devices, exchange(): return lax.all_to_all(cells, axes, split_axis=0, concat_axis=0, tiled=True)  14.2 us
  transfers between devices with their start and end apart: 4, of which 2 were waited for; matrix products, arithmetic and copies ran while one was open for 0% of the time, Pallas kernels for 0%

profile of v1, /device:TPU:1, one launch (start us, length us, event | category | flops | bytes accessed | tf_op | source)
XLA Modules:
  0.0 229.6 jit_solution(11695766642478641055)
XLA Ops:
  0.6 2.7 %route.1 = (s32[128,32]{1,0:T(8,128)}, s32[16,256]{1,0:T(8,128)}) custom-call(s32[16,256]{1,0:T(8,128)} %hist_ref.1), custom_call_target="tpu_custom_call" | custom-call | tf_op jit(solution)/shard_map/route/pallas_call | solution.py:236
  3.4 0.7 add_select_fusion
  4.0 0.1 copy.21
  4.1 0.1 broadcast_in_dim.7
  4.2 0.1 copy.22
  4.3 0.1 broadcast_in_dim.8
  4.4 0.1 reshape.55
  4.4 0.9 copy.23
  5.3 0.1 copy.24
  5.5 20.9 %all_to_all.32 = s32[128,1,40]{2,1,0:T(1,128)S(1)} all-to-all(s32[128,1,40]{2,1,0:T(1,128)S(1)} %bitcast.32), channel_id=1, replica_groups=mesh['batch'=8,'item'=16] {'batch','item'}, dimensions={0} | all-to-all | bytes 40960 | tf_op jit(solution)/shard_map/all_to_all | solution.py:323
  26.3 0.0 copy-start.3
  26.3 4.6 %all-to-all-start.1 = ((bf16[16,4,128,128]{3,2,1,0:T(8,128)(2,1)}), bf16[16,4,128,128]{3,2,1,0:T(8,128)(2,1)S(1)}, u32[]{:S(2)}, u32[]{:S(2)}) async-start(bf16[16,4,128,128]{3,2,1,0:T(8,128)(2,1)} %param.12), calls=%async_computation.1 | async-start | bytes 4194304 | tf_op jit(solution)/shard_map/all_to_all | solution.py:323
  31.0 0.0 copy-done.3
  31.0 0.6 collective-permute-start
  31.5 4.2 %collective-permute-start.1 = (bf16[2048,256]{1,0:T(8,128)(2,1)S(1)}, bf16[2048,256]{1,0:T(8,128)(2,1)}, u32[]{:S(2)}, u32[]{:S(2)}) collective-permute-start(bf16[2048,256]{1,0:T(8,128)(2,1)S(1)} %copy-done.3), channel_id=1, source_target_pairs={{1,0},{2,1},{3,2},{4,3},{5,4},{6,5},{7,6},{8,7},{9,8},{10,9},{11,1... | collective-permute-start | bytes 3145736 | tf_op jit(solution)/shard_map/ppermute | solution.py:342
  35.7 0.1 slice.52
  35.8 0.1 reshape.57.tile_ref
  35.9 0.1 reshape.60.wanted_ref
  36.0 23.0 %collective-permute-done.left_ref = bf16[2048,256]{1,0:T(8,128)(2,1)} collective-permute-done((bf16[2048,256]{1,0:T(8,128)(2,1)S(1)}, bf16[2048,256]{1,0:T(8,128)(2,1)}, u32[]{:S(2)}, u32[]{:S(2)}) %collective-permute-start) | collective-permute-done | bytes 1048608 | tf_op jit(solution)/shard_map/ppermute | solution.py:341
  59.0 0.0 collective-permute-done.1.right_ref
  59.0 0.0 all-to-all-done.1
  59.0 3.6 %graph.1 = bf16[4096,256]{1,0:T(8,128)(2,1)S(1)} custom-call(s32[64]{0:T(128)S(1)} %reshape.57.tile_ref, s32[1]{0:T(128)} %bitcast.3.part_ref, bf16[2048,256]{1,0:T(8,128)(2,1)} %collective-permute-done.left_ref, bf16[2048,256]{1,0:T(8,128)(2,1)S(1)} %copy-done.3, bf16[2048,256]{1,0:T(8,128)(2,1)} %collective-permute-done.1.right_ref, ...), custom_call_target="tpu_custom_call" | custom-call | tf_op jit(solution)/shard_map/graph/pallas_call | solution.py:290
  62.6 0.0 copy-start
  62.6 1.3 copy-done
  63.9 0.0 copy-start.9
  63.9 0.0 copy-start.2
  63.9 0.0 copy-start.4
  64.0 0.0 copy-start.5
  64.0 0.0 copy-start.6
  64.0 0.0 copy-start.7
  64.0 9.5 %all-to-all-start.2 = ((bf16[128,32,256]{2,1,0:T(8,128)(2,1)}), bf16[128,32,256]{2,1,0:T(8,128)(2,1)S(1)}, u32[]{:S(2)}, u32[]{:S(2)}) async-start(bf16[128,32,256]{2,1,0:T(8,128)(2,1)} %bitcast.25), calls=%async_computation.2 | async-start | bytes 4194304 | tf_op jit(solution)/shard_map/all_to_all | solution.py:323
  73.5 0.0 copy-done.9
  73.6 0.0 copy-done.2
  73.6 0.2 copy.26
  73.7 29.3 %all-to-all-done.2 = bf16[128,32,256]{2,1,0:T(8,128)(2,1)S(1)} async-done(((bf16[128,32,256]{2,1,0:T(8,128)(2,1)}), bf16[128,32,256]{2,1,0:T(8,128)(2,1)S(1)}, u32[]{:S(2)}, u32[]{:S(2)}) %all-to-all-start.2) | async-done | bytes 2097184 | tf_op jit(solution)/shard_map/all_to_all | solution.py:323
  103.0 0.0 copy-done.4
  103.0 0.0 copy-done.5
  103.0 0.0 copy-done.6
  103.0 0.0 copy-done.7
  103.1 0.0 copy-start.1
  103.1 1.6 copy-done.1
  104.6 64.3 %shard_map.137 = (bf16[16,256,256]{2,1,0:T(8,128)(2,1)}, bf16[3072,128]{1,0:T(8,128)(2,1)S(1)}) custom-call(s32[16]{0:T(128)S(1)} %copy-done.7, s32[4096]{0:T(1024)S(1)} %bitcast.28, bf16[4096,256]{1,0:T(8,128)(2,1)S(1)} %bitcast.23, bf16[16,256,256]{2,1,0:T(8,128)(2,1)S(1)} %copy-done.1, f32[256,256]{1,0:T(8,128)S(1)} %copy-done.4, f32[1,256]{1,0:T(1,128)S(1)} %bitcast.29, ...), custom_call_target="tpu_custom_call" | custom-call | tf_op jit(solution)/shard_map/pallas_call | solution.py:173
  168.9 38.2 %all_to_all.33.parts_ref = bf16[128,24,128]{2,1,0:T(8,128)(2,1)S(1)} all-to-all(bf16[128,24,128]{2,1,0:T(8,128)(2,1)S(1)} %bitcast.27), channel_id=1, replica_groups=mesh['batch'=8,'item'=16] {'batch','item'}, dimensions={0} | all-to-all | bytes 1572864 | tf_op jit(solution)/shard_map/all_to_all | solution.py:323
  207.2 0.2 sum_spread.1
  207.4 20.4 %all_to_all.34 = bf16[128,24,128]{2,1,0:T(8,128)(2,1)S(1)} all-to-all(bf16[128,24,128]{2,1,0:T(8,128)(2,1)S(1)} %sum_spread.1), channel_id=1, replica_groups=mesh['batch'=8,'item'=16] {'batch','item'}, dimensions={0} | all-to-all | bytes 1572864 | tf_op jit(solution)/shard_map/all_to_all | solution.py:323
  227.7 0.2 bitcast_convert_fusion
  227.9 0.6 slice_bitcast_fusion
  228.6 0.0 copy-start.8
  228.6 1.0 pad_maximum_fusion
  229.5 0.1 copy-done.8
  (9 shorter events, 0.1 us)
Async XLA Ops:
  26.3 4.6 %copy-start.3 = (bf16[2048,256]{1,0:T(8,128)(2,1)S(1)}, bf16[2048,256]{1,0:T(8,128)(2,1)}, u32[]{:S(2)}) copy-start(bf16[2048,256]{1,0:T(8,128)(2,1)} %own_ref.1) | copy-start | bytes 3145732
  26.3 32.6 %all-to-all-start.1 = ((bf16[16,4,128,128]{3,2,1,0:T(8,128)(2,1)}), bf16[16,4,128,128]{3,2,1,0:T(8,128)(2,1)S(1)}, u32[]{:S(2)}, u32[]{:S(2)}) async-start(bf16[16,4,128,128]{3,2,1,0:T(8,128)(2,1)} %param.12), calls=%async_computation.1 | async-start | bytes 4194304 | tf_op jit(solution)/shard_map/all_to_all | solution.py:323
  31.0 28.0 %collective-permute-start = (bf16[2048,256]{1,0:T(8,128)(2,1)S(1)}, bf16[2048,256]{1,0:T(8,128)(2,1)}, u32[]{:S(2)}, u32[]{:S(2)}) collective-permute-start(bf16[2048,256]{1,0:T(8,128)(2,1)S(1)} %copy-done.3), channel_id=1, source_target_pairs={{0,1},{1,2},{2,3},{3,4},{4,5},{5,6},{6,7},{7,8},{8,9},{9,10},{10,1... | collective-permute-start | bytes 3145736 | tf_op jit(solution)/shard_map/ppermute | solution.py:341
  31.5 27.5 %collective-permute-start.1 = (bf16[2048,256]{1,0:T(8,128)(2,1)S(1)}, bf16[2048,256]{1,0:T(8,128)(2,1)}, u32[]{:S(2)}, u32[]{:S(2)}) collective-permute-start(bf16[2048,256]{1,0:T(8,128)(2,1)S(1)} %copy-done.3), channel_id=1, source_target_pairs={{1,0},{2,1},{3,2},{4,3},{5,4},{6,5},{7,6},{8,7},{9,8},{10,9},{11,1... | collective-permute-start | bytes 3145736 | tf_op jit(solution)/shard_map/ppermute | solution.py:342
  62.6 1.3 copy-start
  63.9 9.6 %copy-start.9 = (s32[16,256]{1,0:T(8,128)S(1)}, s32[16,256]{1,0:T(8,128)}, u32[]{:S(2)}) copy-start(s32[16,256]{1,0:T(8,128)} %get-tuple-element.9) | copy-start | bytes 49156
  63.9 9.6 %copy-start.2 = (bf16[256,768]{1,0:T(8,128)(2,1)S(1)}, bf16[256,768]{1,0:T(8,128)(2,1)}, u32[]{:S(2)}) copy-start(bf16[256,768]{1,0:T(8,128)(2,1)} %win_ref.1) | copy-start | bytes 1179652
  63.9 39.1 %copy-start.4 = (f32[256,256]{1,0:T(8,128)S(1)}, f32[256,256]{1,0:T(8,128)}, u32[]{:S(2)}) copy-start(f32[256,256]{1,0:T(8,128)} %pos_ref.1) | copy-start | bytes 786436
  64.0 39.1 %copy-start.5 = (bf16[256,256]{1,0:T(8,128)(2,1)S(1)}, bf16[256,256]{1,0:T(8,128)(2,1)}, u32[]{:S(2)}) copy-start(bf16[256,256]{1,0:T(8,128)(2,1)} %wout_ref.1) | copy-start | bytes 393220
  64.0 39.1 %copy-start.6 = (f32[256]{0:T(256)S(1)}, f32[256]{0:T(256)}, u32[]{:S(2)}) copy-start(f32[256]{0:T(256)} %param.16) | copy-start | bytes 3076
  64.0 39.1 %copy-start.7 = (s32[16]{0:T(128)S(1)}, s32[16]{0:T(128)}, u32[]{:S(2)}) copy-start(s32[16]{0:T(128)} %lens_ref.1) | copy-start | bytes 196
  64.0 39.1 %all-to-all-start.2 = ((bf16[128,32,256]{2,1,0:T(8,128)(2,1)}), bf16[128,32,256]{2,1,0:T(8,128)(2,1)S(1)}, u32[]{:S(2)}, u32[]{:S(2)}) async-start(bf16[128,32,256]{2,1,0:T(8,128)(2,1)} %bitcast.25), calls=%async_computation.2 | async-start | bytes 4194304 | tf_op jit(solution)/shard_map/all_to_all | solution.py:323
  103.1 1.6 copy-start.1
  228.6 1.1 copy-start.8

commit v2 on v1

v2 whole, which is shorter than its diff:
```python
import functools
import math
import jax
import jax.numpy as jnp
from jax import lax
from jax.experimental import pallas as pl
from jax.experimental.pallas import tpu as pltpu
from jax.sharding import PartitionSpec as P

PART_TYPE = jnp.bfloat16
SPREAD_TYPE = jnp.bfloat16
HEADS = 8
BLK = 128
NT = (((1,), (1,)), ((), ()))
TN = (((0,), (0,)), ((), ()))


def dotf(a, b, dims=(((1,), (0,)), ((), ()))):
    return lax.dot_general(a, b, dims, preferred_element_type=jnp.float32)


def diag2(top, low):
    return jnp.concatenate(
        [
            jnp.concatenate([top, jnp.zeros_like(top)], axis=1),
            jnp.concatenate([jnp.zeros_like(low), low], axis=1),
        ],
        axis=0,
    )


def user_pass(
    n, live_len, x_ref, bring, cot_ref, pos_ref, gain_ref, win_ref, wint_ref, wout_ref,
    blk_ref, gin_ref, gout_ref, ggain_ref, gpos_ref, gkt_ref, gvt_ref, mxt_ref, gqt_ref, bias_ref,
):
    feat = pos_ref.shape[1]
    hd = feat // HEADS
    scale = hd ** (-0.5)
    bf = jnp.bfloat16
    resid = jnp.concatenate([x_ref[:n, 0, :], x_ref[:n, 1, :]], axis=1) + pos_ref[:n, :]
    inv = lax.rsqrt(jnp.mean(resid * resid, axis=1, keepdims=True) + 1e-05)
    gain = gain_ref[...]
    rnorm = resid * inv
    normed = (rnorm * gain).astype(bf)
    kv = dotf(normed, win_ref[:, feat:]).astype(bf)
    qkvt = dotf(wint_ref[...], normed, NT).astype(bf)
    live = lax.broadcasted_iota(jnp.int32, (n, feat), 0) < live_len
    gres = jnp.where(live, cot_ref[0, :n, :].astype(jnp.float32), 0.0)
    glow = gres.astype(bf)
    gmt = dotf(wout_ref[...], glow, NT).astype(bf)
    fill = jnp.zeros((2 * hd, 2 * BLK), bf)
    items = [(ib, pair) for ib in range(n // BLK) for pair in range(HEADS // 2)]

    def products(ib, pair):
        r0 = 2 * hd * pair
        quad = 128 * (r0 // 128)
        i0 = ib * BLK
        nj = i0 + BLK
        qd = diag2(qkvt[r0 : r0 + hd, i0:nj], qkvt[r0 + hd : r0 + 2 * hd, i0:nj])
        md = diag2(gmt[r0 : r0 + hd, i0:nj], gmt[r0 + hd : r0 + 2 * hd, i0:nj])
        widen = lambda d: jnp.concatenate([d, fill] if r0 == quad else [fill, d], axis=0)
        sc = dotf(kv[:nj, quad : quad + 128], widen(qd))
        gp = dotf(kv[:nj, feat + quad : feat + quad + 128], widen(md))
        return qd, md, sc, gp

    def soften(ib, pair, made):
        qd, md, sc, gp = made
        i0 = ib * BLK
        edge = sc[i0:] + bias_ref[...]
        sc = edge if ib == 0 else jnp.concatenate([sc[:i0], edge], axis=0)
        top = jnp.max(sc, axis=0, keepdims=True)
        ex = jnp.exp2((sc - top) * (scale * math.log2(math.e)))
        prob = ex * (1.0 / jnp.sum(ex, axis=0, keepdims=True))
        plow = prob.astype(bf)
        inner = jnp.sum(prob * gp, axis=0, keepdims=True)
        gs = (prob * (gp - inner)).astype(bf)
        return qd, md, plow, gs

    def collect(ib, pair, made):
        qd, md, plow, gs = made
        r0 = 2 * hd * pair
        i0 = ib * BLK
        nj = i0 + BLK
        kt = qkvt[feat + r0 : feat + r0 + 2 * hd, :nj]
        vt = qkvt[2 * feat + r0 : 2 * feat + r0 + 2 * hd, :nj]
        mt = dotf(vt, plow)
        gq = dotf(kt, gs)
        gk = dotf(qd, gs, NT) * scale
        gv = dotf(md, plow, NT)
        mxt_ref[r0 : r0 + hd, i0:nj] = mt[:hd, :BLK].astype(bf)
        mxt_ref[r0 + hd : r0 + 2 * hd, i0:nj] = mt[hd:, BLK:].astype(bf)
        gqt_ref[r0 : r0 + hd, i0:nj] = (gq[:hd, :BLK] * scale).astype(bf)
        gqt_ref[r0 + hd : r0 + 2 * hd, i0:nj] = (gq[hd:, BLK:] * scale).astype(bf)
        if n > BLK and ib == 0:
            gkt_ref[r0 : r0 + 2 * hd, :] = gk
            gvt_ref[r0 : r0 + 2 * hd, :] = gv
        else:
            if ib > 0:
                gk = jnp.concatenate([gk[:, :BLK] + gkt_ref[r0 : r0 + 2 * hd, :], gk[:, BLK:]], axis=1)
                gv = jnp.concatenate([gv[:, :BLK] + gvt_ref[r0 : r0 + 2 * hd, :], gv[:, BLK:]], axis=1)
            gqt_ref[feat + r0 : feat + r0 + 2 * hd, :n] = gk.astype(bf)
            gqt_ref[2 * feat + r0 : 2 * feat + r0 + 2 * hd, :n] = gv.astype(bf)

    made, soft = {}, {}
    for t in range(len(items) + 2):
        if t < len(items):
            bring(t, len(items))
            made[t] = products(*items[t])
        if t >= 2:
            collect(*items[t - 2], soft.pop(t - 2))
        s = t - 1
        if 0 <= s < len(items):
            soft[s] = soften(*items[s], made.pop(s))
    mxt = mxt_ref[:, :n]
    attn = dotf(mxt, wout_ref[...], TN)
    blk_ref[0, :n, :] = jnp.where(live, resid + attn, 0.0).astype(bf)
    if n < blk_ref.shape[1]:
        blk_ref[0, n:, :] = jnp.zeros((blk_ref.shape[1] - n, feat), bf)
    gout_ref[...] += dotf(mxt, glow)
    gqkvt = gqt_ref[:, :n]
    gin_ref[...] += dotf(gqkvt, normed)
    gn = dotf(win_ref[...], gqkvt).T
    scaled = gn * gain
    ggain_ref[...] += jnp.sum(gn * rnorm, axis=0, keepdims=True)
    corr = jnp.mean(scaled * resid, axis=1, keepdims=True) * (inv * inv * inv)
    gpos_ref[:n, :] += gres + inv * scaled - resid * corr


def attn_kernel(
    lens_ref, idx_ref, rows_ref, cot_ref, pos_ref, gain_ref, win_ref, wint_ref, wout_ref,
    out_ref, pack_ref, rowf_ref, x_ref, gkt_ref, gvt_ref, mxt_ref, gqt_ref,
    gin_ref, gout_ref, ggain_ref, gpos_ref, bias_ref, held_ref, sems,
):
    users, length, feat = cot_ref.shape

    def bring(user, first, count):
        for t in range(first, first + count, 16):
            some = [rowf_ref[idx_ref[user * length + t + k]] for k in range(16)]
            for k in range(16):
                x_ref[user % 2, t + k] = some[k]

    rowf_ref[:, 0, :] = rows_ref[:, :128].astype(jnp.float32)
    rowf_ref[:, 1, :] = rows_ref[:, 128:].astype(jnp.float32)
    bring(0, 0, length)
    gin_ref[...] = jnp.zeros_like(gin_ref)
    gout_ref[...] = jnp.zeros_like(gout_ref)
    ggain_ref[...] = jnp.zeros_like(ggain_ref)
    gpos_ref[...] = jnp.zeros_like(gpos_ref)
    lane = lax.broadcasted_iota(jnp.int32, (BLK, 2 * BLK), 1)
    row = lax.broadcasted_iota(jnp.int32, (BLK, 2 * BLK), 0)
    bias_ref[...] = jnp.where(row <= (lane & (BLK - 1)), 0.0, -1e30)

    def put(u):
        return pltpu.make_async_copy(held_ref.at[u % 2], out_ref.at[u], sems.at[u % 2])

    def step(u, carry):
        live_len = lens_ref[u]
        coming = jnp.minimum(u + 1, users - 1)

        @pl.when(u >= 2)
        def _():
            put(u - 2).wait()

        def run(n):
            user_pass(
                n, live_len, x_ref.at[u % 2],
                lambda t, of: bring(coming, t * length // of, length // of),
                cot_ref.at[pl.ds(u, 1)], pos_ref, gain_ref, win_ref, wint_ref, wout_ref,
                held_ref.at[pl.ds(u % 2, 1)], gin_ref, gout_ref, ggain_ref, gpos_ref,
                gkt_ref, gvt_ref, mxt_ref, gqt_ref, bias_ref,
            )

        @pl.when(live_len <= BLK)
        def _():
            run(BLK)

        @pl.when(live_len > BLK)
        def _():
            run(length)

        put(u).start()
        return carry

    lax.fori_loop(0, users, step, 0)
    gin = gin_ref[...].T
    at = 0
    for whole in (gin, gout_ref[...], gpos_ref[...]):
        for c in range(whole.shape[1] // 128):
            pack_ref[at : at + feat, :] = whole[:, 128 * c : 128 * c + 128].astype(pack_ref.dtype)
            at += feat
    tail = pack_ref.shape[0] - at
    pack_ref[at:, :] = jnp.zeros((tail, 128), pack_ref.dtype)
    top_row = lax.broadcasted_iota(jnp.int32, (16, 128), 0)
    gg = ggain_ref[...]
    both = jnp.where(top_row == 0, gg[:, :128], jnp.where(top_row == 1, gg[:, 128:], 0.0))
    pack_ref[at : at + 16, :] = both.astype(pack_ref.dtype)
    put(users - 2).wait()
    put(users - 1).wait()


def attention(rows, idx, lengths, cot, position, gain, win, wint, wout, pack_rows, pack_type):
    users, length, feat = cot.shape
    f32, bf = jnp.float32, jnp.bfloat16
    scalars = pl.BlockSpec(memory_space=pltpu.SMEM)
    near = pl.BlockSpec(memory_space=pltpu.VMEM)
    return pl.pallas_call(
        attn_kernel,
        out_shape=(
            jax.ShapeDtypeStruct((users, length, feat), bf),
            jax.ShapeDtypeStruct((pack_rows, 128), pack_type),
        ),
        in_specs=[scalars, scalars] + [near] * 7,
        out_specs=(pl.BlockSpec(memory_space=pl.ANY), near),
        scratch_shapes=[
            pltpu.VMEM((rows.shape[0], 2, 128), f32),
            pltpu.VMEM((2, length, 2, 128), f32),
            pltpu.VMEM((feat, BLK), f32),
            pltpu.VMEM((feat, BLK), f32),
            pltpu.VMEM((feat, length), bf),
            pltpu.VMEM((3 * feat, length), bf),
            pltpu.VMEM((3 * feat, feat), f32),
            pltpu.VMEM((feat, feat), f32),
            pltpu.VMEM((1, feat), f32),
            pltpu.VMEM((length, feat), f32),
            pltpu.VMEM((BLK, 2 * BLK), f32),
            pltpu.VMEM((2, length, feat), bf),
            pltpu.SemaphoreType.DMA((2,)),
        ],
        compiler_params=pltpu.CompilerParams(vmem_limit_bytes=40 * 2**20),
        name="attention",
    )(lengths, idx, rows, cot, position, gain.reshape(1, feat), win, wint, wout)


def route_kernel(n_batch, n_item, hist_ref, sent_ref, place_ref):
    users, length = hist_ref.shape
    peers, per_peer = sent_ref.shape
    rows_own = 256
    f32, bf = jnp.float32, jnp.bfloat16
    peer_row = lax.broadcasted_iota(jnp.int32, (peers, length), 0)
    slot_row = lax.broadcasted_iota(jnp.int32, (per_peer, length), 0)
    before = (
        lax.broadcasted_iota(jnp.int32, (length, length), 0)
        < lax.broadcasted_iota(jnp.int32, (length, length), 1)
    ).astype(f32).astype(bf)
    counts = jnp.zeros((peers, 1), f32)
    sent = jnp.zeros((peers, per_peer), f32)
    for u in range(users):
        ids = hist_ref[u : u + 1, :]
        run = ids // rows_own
        owner = (run % n_batch) * n_item + run // n_batch
        inside = (ids % rows_own).astype(f32)
        mine = (peer_row == owner).astype(f32)
        ahead = dotf(mine.astype(bf), before) + counts
        rank = jnp.sum(mine * ahead, axis=0, keepdims=True)
        counts = counts + jnp.sum(mine, axis=1, keepdims=True)
        rank_int = rank.astype(jnp.int32)
        place_ref[u : u + 1, :] = owner * per_peer + rank_int
        slot = (slot_row == rank_int).astype(f32).astype(bf)
        sent = sent + dotf((mine * inside).astype(bf), slot, NT)
    sent_ref[...] = sent.astype(jnp.int32)


def route(history, n_batch, n_item):
    users, length = history.shape
    peers = n_batch * n_item
    per_peer = users * length // peers
    return pl.pallas_call(
        functools.partial(route_kernel, n_batch, n_item),
        out_shape=(
            jax.ShapeDtypeStruct((peers, per_peer), jnp.int32),
            jax.ShapeDtypeStruct((users, length), jnp.int32),
        ),
        name="route",
    )(history)


def graph_kernel(
    tile_ref, part_ref, left_ref, own_ref, right_ref, held_ref, *refs
):
    arrived_refs = refs[: -5]
    wanted_ref, found_ref, table, weights_ref, sems = refs[-5:]
    rows_item, feat = own_ref.shape
    tile = weights_ref.shape[-1]
    groups, row_tiles, slots = weights_ref.shape[:3]
    part = part_ref[0]
    moves = [
        (src, table.at[pl.ds(i * rows_item, rows_item)])
        for i, src in enumerate((left_ref, own_ref, right_ref))
    ]
    moves.append((held_ref.at[pl.ds(part * row_tiles, row_tiles)], weights_ref.at[part]))
    for k, src in enumerate(arrived_refs):
        moves.append((src, weights_ref.at[lax.rem(part + groups - 1 - k, groups)]))
    copies = [
        pltpu.make_async_copy(src, dst, sems.at[i]) for i, (src, dst) in enumerate(moves)
    ]
    for c in copies:
        c.start()
    for c in copies:
        c.wait()

    def tile_of(g, n, k):
        place = tile_ref[(g * row_tiles + n) * slots + k]
        return table[pl.ds(pl.multiple_of(place * tile, tile), tile), :]

    halves = []
    for n in range(row_tiles):
        acc = jnp.zeros((tile, feat), jnp.float32)
        for g in range(groups):
            for k in range(0, slots, 2):
                lhs = jnp.concatenate([weights_ref[g, n, k], weights_ref[g, n, k + 1]], axis=1)
                rhs = jnp.concatenate([tile_of(g, n, k), tile_of(g, n, k + 1)], axis=0)
                acc = acc + dotf(lhs, rhs)
        start = pl.multiple_of(rows_item + (part * row_tiles + n) * tile, tile)
        own = table[pl.ds(start, tile), :].astype(jnp.float32)
        halves.append((0.5 * (own + acc)).astype(jnp.bfloat16))
    propagated = jnp.concatenate(halves, axis=0)
    columns = wanted_ref[...].astype(jnp.float32).T
    spot = lax.broadcasted_iota(jnp.int32, (128, row_tiles * tile), 1).astype(jnp.float32)
    for b in range(columns.shape[1]):
        pick = (columns[:, b : b + 1] == spot).astype(jnp.float32).astype(jnp.bfloat16)
        found_ref[128 * b : 128 * b + 128, :] = dotf(pick, propagated).astype(jnp.bfloat16)


def graph(tile_ids, part, left, own, right, held, arrived, wanted):
    rows_item, feat = own.shape
    count = wanted.shape[0] * wanted.shape[1]
    anywhere = pl.BlockSpec(memory_space=pl.ANY)
    scalars = pl.BlockSpec(memory_space=pltpu.SMEM)
    near = pl.BlockSpec(memory_space=pltpu.VMEM)
    block = arrived[0].shape
    return pl.pallas_call(
        graph_kernel,
        out_shape=jax.ShapeDtypeStruct((count, feat), jnp.bfloat16),
        in_specs=[scalars, scalars] + [anywhere] * (4 + len(arrived)) + [near],
        out_specs=near,
        scratch_shapes=[
            pltpu.VMEM((3 * rows_item, feat), jnp.bfloat16),
            pltpu.VMEM((1 + len(arrived),) + block, jnp.bfloat16),
            pltpu.SemaphoreType.DMA((4 + len(arrived),)),
        ],
        compiler_params=pltpu.CompilerParams(vmem_limit_bytes=40 * 2**20),
        name="graph",
    )(tile_ids, part, left, own, right, held, *arrived, wanted)


def sum_kernel(parts_ref, out_ref):
    total = jnp.sum(parts_ref[...].astype(jnp.float32), axis=0, keepdims=True)
    out_ref[...] = jnp.broadcast_to(total, out_ref.shape).astype(out_ref.dtype)


def sum_spread(parts, spread_type):
    return pl.pallas_call(
        sum_kernel,
        out_shape=jax.ShapeDtypeStruct(parts.shape, spread_type),
        compiler_params=pltpu.CompilerParams(vmem_limit_bytes=40 * 2**20),
        name="sum_spread",
    )(parts)


def exchange(cells, axes):
    return lax.all_to_all(cells, axes, split_axis=0, concat_axis=0, tiled=True)


def local(
    item_table, neighbours, tile_weights, history, lengths, position, norm_gain,
    in_weight, out_weight, cotangent,
):
    n_batch = lax.axis_size("batch")
    n_item = lax.axis_size("item")
    peers = n_batch * n_item
    everyone = ("batch", "item")
    rows_item, feat = item_table.shape
    tile = tile_weights.shape[2]
    tiles_here = rows_item // tile
    slots = tile_weights.shape[1]
    row_tiles = tiles_here // n_batch
    here = lax.axis_index("item")
    users_here, length = history.shape
    left = lax.ppermute(item_table, "item", [(i, (i + 1) % n_item) for i in range(n_item)])
    right = lax.ppermute(item_table, "item", [((i + 1) % n_item, i) for i in range(n_item)])
    mine = lax.axis_index("batch")
    arrived = []
    for k in range(1, n_batch):
        block = lax.dynamic_slice_in_dim(
            tile_weights, lax.rem(mine + k, n_batch) * row_tiles, row_tiles, 0
        )
        arrived.append(
            lax.ppermute(block, "batch", [(i, (i + k) % n_batch) for i in range(n_batch)])
        )
    sent, place = route(history, n_batch, n_item)
    per_peer = sent.shape[1]
    rim = jnp.mod(neighbours - (here - 1) * tiles_here, n_item * tiles_here)
    rim = jnp.broadcast_to(
        rim.reshape(n_batch, 1, row_tiles * slots), (n_batch, n_item, row_tiles * slots)
    ).reshape(peers, row_tiles * slots)
    got = exchange(jnp.concatenate([sent, rim], axis=1), everyone)
    wanted = got[:, :per_peer].reshape(-1, 128)
    tile_ids = lax.dynamic_index_in_dim(
        got[:, per_peer:].reshape(n_batch, n_item, row_tiles * slots), here, 1, keepdims=False
    ).reshape(-1)
    found = graph(tile_ids, mine.reshape(1), left, item_table, right, tile_weights, arrived, wanted)
    rows = exchange(found.reshape(peers, per_peer, feat), everyone).reshape(-1, feat)
    pack_rows = peers * 24
    block_out, packed = attention(
        rows, place.reshape(-1), lengths, cotangent, position, norm_gain, in_weight,
        in_weight.T, out_weight, pack_rows, PART_TYPE,
    )
    parts = exchange(packed.reshape(peers, pack_rows // peers, 128), everyone)
    full = exchange(sum_spread(parts, SPREAD_TYPE), everyone).reshape(pack_rows, 128)
    full = full.astype(jnp.float32)
    slab = lambda a, b: jnp.concatenate(
        [full[feat * i : feat * i + feat] for i in range(a, b)], axis=1
    )
    gain_row = 10 * feat
    return (
        block_out,
        slab(0, 6),
        slab(6, 8),
        full[gain_row : gain_row + 2].reshape(feat),
        slab(8, 10),
    )


def solution(mesh):
    in_specs = (
        P("item", None),
        P("item", "batch"),
        P("item", "batch", None, None),
        P(("batch", "item"), None),
        P(("batch", "item")),
        P(),
        P(),
        P(),
        P(),
        P(("batch", "item"), None, None),
    )
    out_specs = (P(("batch", "item"), None, None), P(), P(), P(), P())
    return jax.shard_map(local, mesh=mesh, in_specs=in_specs, out_specs=out_specs, check_vma=False)
```

time: 229 us -> 195 us (0.85)
  blocking collectives: 79.5 us -> 45.8 us
  Pallas kernels: 70.8 us -> 56.9 us
  waiting for transfers between devices: 52.3 us -> 58.9 us
  starting transfers between devices: 18.9 us -> 23.6 us
    all_to_all x3 -> x2, blocking collectives: 79.5 us -> 45.8 us  [exchange(): return lax.all_to_all(cells, axes, split_axis=0, concat_axis=0, tiled=True)]
    ppermute x1, waiting for transfers between devices: 23 us -> 0.01 us  [local(): lax.ppermute(item_table, 'item', [(i, (i + 1) % n_item) for i in range(n_...]
    ppermute x0 -> x7, waiting for transfers between devices: none -> 20 us  [local(): lax.ppermute(block, 'batch', [(i, (i + k) % n_batch) for i in range(n_bat...]
    pallas_call x1, Pallas kernels: 64.3 us -> 48.5 us  [attention(): pl.pallas_call(attn_kernel, out_shape=(jax.ShapeDtypeStruct((users, lengt...]
    all_to_all x2, waiting for transfers between devices: 29.3 us -> 38.9 us  [exchange(): return lax.all_to_all(cells, axes, split_axis=0, concat_axis=0, tiled=True)]
    ppermute x0 -> x7, starting transfers between devices: none -> 7.28 us  [local(): lax.ppermute(block, 'batch', [(i, (i + k) % n_batch) for i in range(n_bat...]
    all_to_all x2, starting transfers between devices: 14.2 us -> 9.13 us  [exchange(): return lax.all_to_all(cells, axes, split_axis=0, concat_axis=0, tiled=True)]
    dynamic_slice x0 -> x1, local copies, waits for them, and re-layouts: none -> 2.73 us  [local(): lax.dynamic_slice_in_dim(tile_weights, lax.rem(mine + k, n_batch) * row_t...]
  transfers between devices with their start and end apart: 4 -> 11, of which waited for: 2 -> 6; matrix products, arithmetic and copies ran while one was open for 0% -> 3% of each run, Pallas kernels for 0% -> 1%
where the time goes in v2:
time: 195 us
  waiting for transfers between devices  58.9 us (30%)
  Pallas kernels  56.9 us (29%)
  blocking collectives  45.8 us (23%)
  starting transfers between devices  23.6 us (12%)
  local copies, waits for them, and re-layouts  7.66 us (4%)
    pallas_call x1, Pallas kernels, attention(): pl.pallas_call(attn_kernel, out_shape=(jax.ShapeDtypeStruct((users, lengt...  48.5 us
    all_to_all x2, blocking collectives, exchange(): return lax.all_to_all(cells, axes, split_axis=0, concat_axis=0, tiled=True)  45.8 us
    all_to_all x2, waiting for transfers between devices, exchange(): return lax.all_to_all(cells, axes, split_axis=0, concat_axis=0, tiled=True)  38.9 us
    ppermute x7, waiting for transfers between devices, local(): lax.ppermute(block, 'batch', [(i, (i + k) % n_batch) for i in range(n_bat...  20 us
    all_to_all x2, starting transfers between devices, exchange(): return lax.all_to_all(cells, axes, split_axis=0, concat_axis=0, tiled=True)  9.13 us
    ppermute x7, starting transfers between devices, local(): lax.ppermute(block, 'batch', [(i, (i + k) % n_batch) for i in range(n_bat...  7.28 us
    pallas_call x1, Pallas kernels, graph(): pl.pallas_call(graph_kernel, out_shape=jax.ShapeDtypeStruct((count, feat)...  5.48 us
    ppermute x1, starting transfers between devices, local(): lax.ppermute(item_table, 'item', [((i + 1) % n_item, i) for i in range(n_...  4.65 us
  transfers between devices with their start and end apart: 11, of which 6 were waited for; matrix products, arithmetic and copies ran while one was open for 3% of the time, Pallas kernels for 1%

profile of v2, /device:TPU:1, one launch (start us, length us, event | category | flops | bytes accessed | tf_op | source)
XLA Modules:
  0.0 194.7 jit_solution(12808977540602561853)
XLA Ops:
  0.6 2.5 %collective-permute-start = (bf16[2048,256]{1,0:T(8,128)(2,1)}, bf16[2048,256]{1,0:T(8,128)(2,1)}, u32[]{:S(2)}, u32[]{:S(2)}) collective-permute-start(bf16[2048,256]{1,0:T(8,128)(2,1)} %own_ref.1), channel_id=1, source_target_pairs={{0,1},{1,2},{2,3},{3,4},{4,5},{5,6},{6,7},{7,8},{8,9},{9,10},{10,1... | collective-permute-start | bytes 3145736 | tf_op jit(solution)/shard_map/ppermute | solution.py:379
  3.2 4.7 %collective-permute-start.1 = (bf16[2048,256]{1,0:T(8,128)(2,1)}, bf16[2048,256]{1,0:T(8,128)(2,1)}, u32[]{:S(2)}, u32[]{:S(2)}) collective-permute-start(bf16[2048,256]{1,0:T(8,128)(2,1)} %own_ref.1), channel_id=1, source_target_pairs={{1,0},{2,1},{3,2},{4,3},{5,4},{6,5},{7,6},{8,7},{9,8},{10,9},{11,1... | collective-permute-start | bytes 3145736 | tf_op jit(solution)/shard_map/ppermute | solution.py:380
  7.8 0.0 copy-start.10
  7.8 0.0 copy-start
  7.8 2.7 %constant_dynamic-slice_fusion = (bf16[2,4,128,128]{3,2,1,0:T(8,128)(2,1)}, bf16[2,4,128,128]{3,2,1,0:T(8,128)(2,1)}, bf16[2,4,128,128]{3,2,1,0:T(8,128)(2,1)}, ...) fusion(bf16[16,4,128,128]{3,2,1,0:T(8,128)(2,1)} %held_ref.1, ...), kind=kLoop, calls=%fused_computation.14 | loop fusion | bytes 3670044 | tf_op jit(solution)/shard_map/dynamic_slice | solution.py:384
  10.6 2.1 %collective-permute-start.2 = (bf16[2,4,128,128]{3,2,1,0:T(8,128)(2,1)S(1)}, bf16[2,4,128,128]{3,2,1,0:T(8,128)(2,1)S(1)}, u32[]{:S(2)}, u32[]{:S(2)}) collective-permute-start(bf16[2,4,128,128]{3,2,1,0:T(8,128)(2,1)S(1)} %get-tuple-element.19), channel_id=1, source_target_pairs={{0,16},{16,32},{32,48},{48,64},{64,80},{80,96},{96,112},{112,0},{1... | collective-permute-start | bytes 786440 | tf_op jit(solution)/shard_map/ppermute | solution.py:388
  12.6 1.2 collective-permute-start.3
  13.8 1.6 collective-permute-start.4
  15.4 2.6 %collective-permute-done.2.refs_0_ = bf16[2,4,128,128]{3,2,1,0:T(8,128)(2,1)S(1)} collective-permute-done((bf16[2,4,128,128]{3,2,1,0:T(8,128)(2,1)S(1)}, bf16[2,4,128,128]{3,2,1,0:T(8,128)(2,1)S(1)}, u32[]{:S(2)}, u32[]{:S(2)}) %collective-permute-start.2) | collective-permute-done | bytes 262176 | tf_op jit(solution)/shard_map/ppermute | solution.py:388
  17.9 2.5 %collective-permute-start.5 = (bf16[2,4,128,128]{3,2,1,0:T(8,128)(2,1)}, bf16[2,4,128,128]{3,2,1,0:T(8,128)(2,1)}, u32[]{:S(2)}, u32[]{:S(2)}) collective-permute-start(bf16[2,4,128,128]{3,2,1,0:T(8,128)(2,1)} %get-tuple-element.16), channel_id=1, source_target_pairs={{0,64},{16,80},{32,96},{48,112},{64,0},{80,16},{96,32},{112,48},{1... | collective-permute-start | bytes 786440 | tf_op jit(solution)/shard_map/ppermute | solution.py:388
  20.4 5.5 %collective-permute-done.3.refs_1_ = bf16[2,4,128,128]{3,2,1,0:T(8,128)(2,1)} collective-permute-done((bf16[2,4,128,128]{3,2,1,0:T(8,128)(2,1)}, bf16[2,4,128,128]{3,2,1,0:T(8,128)(2,1)}, u32[]{:S(2)}, u32[]{:S(2)}) %collective-permute-start.3) | collective-permute-done | bytes 262176 | tf_op jit(solution)/shard_map/ppermute | solution.py:388
  25.9 0.0 collective-permute-start.6
  25.9 3.4 %collective-permute-done.4.refs_2_ = bf16[2,4,128,128]{3,2,1,0:T(8,128)(2,1)} collective-permute-done((bf16[2,4,128,128]{3,2,1,0:T(8,128)(2,1)}, bf16[2,4,128,128]{3,2,1,0:T(8,128)(2,1)}, u32[]{:S(2)}, u32[]{:S(2)}) %collective-permute-start.4) | collective-permute-done | bytes 262176 | tf_op jit(solution)/shard_map/ppermute | solution.py:388
  29.3 0.0 collective-permute-start.7
  29.3 8.5 %collective-permute-done.5.refs_3_ = bf16[2,4,128,128]{3,2,1,0:T(8,128)(2,1)} collective-permute-done((bf16[2,4,128,128]{3,2,1,0:T(8,128)(2,1)}, bf16[2,4,128,128]{3,2,1,0:T(8,128)(2,1)}, u32[]{:S(2)}, u32[]{:S(2)}) %collective-permute-start.5) | collective-permute-done | bytes 262176 | tf_op jit(solution)/shard_map/ppermute | solution.py:388
  37.8 0.0 collective-permute-start.8
  37.8 0.0 copy-done.10
  37.8 2.7 %route.1 = (s32[128,32]{1,0:T(8,128)}, s32[16,256]{1,0:T(8,128)}) custom-call(s32[16,256]{1,0:T(8,128)} %hist_ref.1), custom_call_target="tpu_custom_call" | custom-call | tf_op jit(solution)/shard_map/route/pallas_call | solution.py:267
  40.5 0.1 copy.21
  40.6 0.1 broadcast_in_dim.7
  40.7 0.1 copy.22
  40.8 0.1 broadcast_in_dim.8
  40.8 0.1 reshape.52
  40.9 0.9 copy.23
  41.8 0.8 copy.24
  42.6 4.6 %all-to-all-start = ((s32[128,1,40]{2,1,0:T(1,128)}), s32[128,1,40]{2,1,0:T(1,128)S(1)}, u32[]{:S(2)}, u32[]{:S(2)}) async-start(s32[128,1,40]{2,1,0:T(1,128)} %bitcast), calls=%async_computation | async-start | bytes 131072 | tf_op jit(solution)/shard_map/all_to_all | solution.py:361
  47.1 9.5 %all-to-all-done = s32[128,1,40]{2,1,0:T(1,128)S(1)} async-done(((s32[128,1,40]{2,1,0:T(1,128)}), s32[128,1,40]{2,1,0:T(1,128)S(1)}, u32[]{:S(2)}, u32[]{:S(2)}) %all-to-all-start) | async-done | bytes 20512 | tf_op jit(solution)/shard_map/all_to_all | solution.py:361
  56.6 0.1 slice.52
  56.7 0.1 reshape.54.tile_ref
  56.8 0.1 reshape.56.refs_7_
  56.9 0.0 collective-permute-done.6.refs_4_
  56.9 0.0 collective-permute-done.7.refs_5_
  56.9 0.0 collective-permute-done.8.refs_6_
  56.9 0.0 collective-permute-done.left_ref
  56.9 0.0 collective-permute-done.1.right_ref
  56.9 0.0 copy-done
  57.0 0.0 copy-done.3
  57.0 5.5 %graph.1 = bf16[4096,256]{1,0:T(8,128)(2,1)} custom-call(s32[64]{0:T(128)S(1)} %reshape.54.tile_ref, s32[1]{0:T(128)} %bitcast.3.part_ref, bf16[2048,256]{1,0:T(8,128)(2,1)} %collective-permute-done.left_ref, bf16[2048,256]{1,0:T(8,128)(2,1)S(1)} %copy-done.3, bf16[2048,256]{1,0:T(8,128)(2,1)} %collective-permute-done.1.right_ref, ...), custom_call_target="tpu_custom_call" | custom-call | tf_op jit(solution)/shard_map/graph/pallas_call | solution.py:331
  62.5 0.0 copy-start.9
  62.5 0.0 copy-start.2
  62.5 0.0 copy-start.4
  62.5 0.0 copy-start.5
  62.5 0.0 copy-start.6
  62.5 0.0 copy-start.7
  62.5 4.6 %all-to-all-start.1 = ((bf16[128,32,256]{2,1,0:T(8,128)(2,1)}), bf16[128,32,256]{2,1,0:T(8,128)(2,1)S(1)}, u32[]{:S(2)}, u32[]{:S(2)}) async-start(bf16[128,32,256]{2,1,0:T(8,128)(2,1)} %bitcast.4), calls=%async_computation.1 | async-start | bytes 4194304 | tf_op jit(solution)/shard_map/all_to_all | solution.py:361
  67.1 0.0 copy-done.9
  67.1 0.0 copy-done.2
  67.1 0.2 copy.26
  67.3 29.4 %all-to-all-done.1 = bf16[128,32,256]{2,1,0:T(8,128)(2,1)S(1)} async-done(((bf16[128,32,256]{2,1,0:T(8,128)(2,1)}), bf16[128,32,256]{2,1,0:T(8,128)(2,1)S(1)}, u32[]{:S(2)}, u32[]{:S(2)}) %all-to-all-start.1) | async-done | bytes 2097184 | tf_op jit(solution)/shard_map/all_to_all | solution.py:361
  96.7 0.0 copy-done.4
  96.7 0.0 copy-done.5
  96.7 0.0 copy-done.6
  96.7 0.0 copy-done.7
  96.8 0.0 copy-start.1
  96.8 1.6 copy-done.1
  98.4 48.5 %attention.1 = (bf16[16,256,256]{2,1,0:T(8,128)(2,1)}, bf16[3072,128]{1,0:T(8,128)(2,1)S(1)}) custom-call(s32[16]{0:T(128)S(1)} %copy-done.7, s32[4096]{0:T(1024)S(1)} %bitcast.25, bf16[4096,256]{1,0:T(8,128)(2,1)S(1)} %bitcast.22, bf16[16,256,256]{2,1,0:T(8,128)(2,1)S(1)} %copy-done.1, f32[256,256]{1,0:T(8,128)S(1)} %copy-done.4, f32[1,256]{1,0:T(1,128)S(1)} %bitcast.26, ...), custom_call_target="tpu_custom_call" | custom-call | tf_op jit(solution)/shard_map/attention/pallas_call | solution.py:206
  146.8 25.4 %all_to_all.27.parts_ref = bf16[128,24,128]{2,1,0:T(8,128)(2,1)S(1)} all-to-all(bf16[128,24,128]{2,1,0:T(8,128)(2,1)S(1)} %bitcast.24), channel_id=1, replica_groups=mesh['batch'=8,'item'=16] {'batch','item'}, dimensions={0} | all-to-all | bytes 1572864 | tf_op jit(solution)/shard_map/all_to_all | solution.py:361
  172.3 0.2 sum_spread.1
  172.5 20.4 %all_to_all.28 = bf16[128,24,128]{2,1,0:T(8,128)(2,1)S(1)} all-to-all(bf16[128,24,128]{2,1,0:T(8,128)(2,1)S(1)} %sum_spread.1), channel_id=1, replica_groups=mesh['batch'=8,'item'=16] {'batch','item'}, dimensions={0} | all-to-all | bytes 1572864 | tf_op jit(solution)/shard_map/all_to_all | solution.py:361
  192.8 0.2 bitcast_convert_fusion
  193.0 0.6 slice_bitcast_fusion
  193.7 0.0 copy-start.8
  193.7 0.9 pad_maximum_fusion
  194.6 0.2 copy-done.8
  (11 shorter events, 0.1 us)
Async XLA Ops:
  0.6 56.3 %collective-permute-start = (bf16[2048,256]{1,0:T(8,128)(2,1)}, bf16[2048,256]{1,0:T(8,128)(2,1)}, u32[]{:S(2)}, u32[]{:S(2)}) collective-permute-start(bf16[2048,256]{1,0:T(8,128)(2,1)} %own_ref.1), channel_id=1, source_target_pairs={{0,1},{1,2},{2,3},{3,4},{4,5},{5,6},{6,7},{7,8},{8,9},{9,10},{10,1... | collective-permute-start | bytes 3145736 | tf_op jit(solution)/shard_map/ppermute | solution.py:379
  3.2 53.8 %collective-permute-start.1 = (bf16[2048,256]{1,0:T(8,128)(2,1)}, bf16[2048,256]{1,0:T(8,128)(2,1)}, u32[]{:S(2)}, u32[]{:S(2)}) collective-permute-start(bf16[2048,256]{1,0:T(8,128)(2,1)} %own_ref.1), channel_id=1, source_target_pairs={{1,0},{2,1},{3,2},{4,3},{5,4},{6,5},{7,6},{8,7},{9,8},{10,9},{11,1... | collective-permute-start | bytes 3145736 | tf_op jit(solution)/shard_map/ppermute | solution.py:380
  7.8 30.0 %copy-start.10 = (s32[16,4]{0,1:T(4,128)S(1)}, s32[16,4]{0,1:T(4,128)}, u32[]{:S(2)}) copy-start(s32[16,4]{0,1:T(4,128)} %param.11) | copy-start | bytes 772
  7.8 49.1 %copy-start = (bf16[16,4,128,128]{3,2,1,0:T(8,128)(2,1)S(1)}, bf16[16,4,128,128]{3,2,1,0:T(8,128)(2,1)}, u32[]{:S(2)}) copy-start(bf16[16,4,128,128]{3,2,1,0:T(8,128)(2,1)} %held_ref.1) | copy-start | bytes 6291460
  7.8 49.1 %copy-start.3 = (bf16[2048,256]{1,0:T(8,128)(2,1)S(1)}, bf16[2048,256]{1,0:T(8,128)(2,1)}, u32[]{:S(2)}) copy-start(bf16[2048,256]{1,0:T(8,128)(2,1)} %own_ref.1) | copy-start | bytes 3145732
  10.6 7.4 %collective-permute-start.2 = (bf16[2,4,128,128]{3,2,1,0:T(8,128)(2,1)S(1)}, bf16[2,4,128,128]{3,2,1,0:T(8,128)(2,1)S(1)}, u32[]{:S(2)}, u32[]{:S(2)}) collective-permute-start(bf16[2,4,128,128]{3,2,1,0:T(8,128)(2,1)S(1)} %get-tuple-element.19), channel_id=1, source_target_pairs={{0,16},{16,32},{32,48},{48,64},{64,80},{80,96},{96,112},{112,0},{1... | collective-permute-start | bytes 786440 | tf_op jit(solution)/shard_map/ppermute | solution.py:388
  12.6 13.3 %collective-permute-start.3 = (bf16[2,4,128,128]{3,2,1,0:T(8,128)(2,1)}, bf16[2,4,128,128]{3,2,1,0:T(8,128)(2,1)}, u32[]{:S(2)}, u32[]{:S(2)}) collective-permute-start(bf16[2,4,128,128]{3,2,1,0:T(8,128)(2,1)} %get-tuple-element.18), channel_id=1, source_target_pairs={{0,32},{16,48},{32,64},{48,80},{64,96},{80,112},{96,0},{112,16},{1... | collective-permute-start | bytes 786440 | tf_op jit(solution)/shard_map/ppermute | solution.py:388
  13.8 15.5 %collective-permute-start.4 = (bf16[2,4,128,128]{3,2,1,0:T(8,128)(2,1)}, bf16[2,4,128,128]{3,2,1,0:T(8,128)(2,1)}, u32[]{:S(2)}, u32[]{:S(2)}) collective-permute-start(bf16[2,4,128,128]{3,2,1,0:T(8,128)(2,1)} %get-tuple-element.17), channel_id=1, source_target_pairs={{0,48},{16,64},{32,80},{48,96},{64,112},{80,0},{96,16},{112,32},{1... | collective-permute-start | bytes 786440 | tf_op jit(solution)/shard_map/ppermute | solution.py:388
  17.9 19.8 %collective-permute-start.5 = (bf16[2,4,128,128]{3,2,1,0:T(8,128)(2,1)}, bf16[2,4,128,128]{3,2,1,0:T(8,128)(2,1)}, u32[]{:S(2)}, u32[]{:S(2)}) collective-permute-start(bf16[2,4,128,128]{3,2,1,0:T(8,128)(2,1)} %get-tuple-element.16), channel_id=1, source_target_pairs={{0,64},{16,80},{32,96},{48,112},{64,0},{80,16},{96,32},{112,48},{1... | collective-permute-start | bytes 786440 | tf_op jit(solution)/shard_map/ppermute | solution.py:388
  25.9 31.0 %collective-permute-start.6 = (bf16[2,4,128,128]{3,2,1,0:T(8,128)(2,1)}, bf16[2,4,128,128]{3,2,1,0:T(8,128)(2,1)}, u32[]{:S(2)}, u32[]{:S(2)}) collective-permute-start(bf16[2,4,128,128]{3,2,1,0:T(8,128)(2,1)} %get-tuple-element.15), channel_id=1, source_target_pairs={{0,80},{16,96},{32,112},{48,0},{64,16},{80,32},{96,48},{112,64},{1... | collective-permute-start | bytes 786440 | tf_op jit(solution)/shard_map/ppermute | solution.py:388
  29.3 27.6 %collective-permute-start.7 = (bf16[2,4,128,128]{3,2,1,0:T(8,128)(2,1)}, bf16[2,4,128,128]{3,2,1,0:T(8,128)(2,1)}, u32[]{:S(2)}, u32[]{:S(2)}) collective-permute-start(bf16[2,4,128,128]{3,2,1,0:T(8,128)(2,1)} %get-tuple-element.14), channel_id=1, source_target_pairs={{0,96},{16,112},{32,0},{48,16},{64,32},{80,48},{96,64},{112,80},{1... | collective-permute-start | bytes 786440 | tf_op jit(solution)/shard_map/ppermute | solution.py:388
  37.8 19.1 %collective-permute-start.8 = (bf16[2,4,128,128]{3,2,1,0:T(8,128)(2,1)}, bf16[2,4,128,128]{3,2,1,0:T(8,128)(2,1)}, u32[]{:S(2)}, u32[]{:S(2)}) collective-permute-start(bf16[2,4,128,128]{3,2,1,0:T(8,128)(2,1)} %get-tuple-element.13), channel_id=1, source_target_pairs={{0,112},{16,0},{32,16},{48,32},{64,48},{80,64},{96,80},{112,96},{1... | collective-permute-start | bytes 786440 | tf_op jit(solution)/shard_map/ppermute | solution.py:388
  42.6 14.1 %all-to-all-start = ((s32[128,1,40]{2,1,0:T(1,128)}), s32[128,1,40]{2,1,0:T(1,128)S(1)}, u32[]{:S(2)}, u32[]{:S(2)}) async-start(s32[128,1,40]{2,1,0:T(1,128)} %bitcast), calls=%async_computation | async-start | bytes 131072 | tf_op jit(solution)/shard_map/all_to_all | solution.py:361
  62.5 4.7 %copy-start.9 = (s32[16,256]{1,0:T(8,128)S(1)}, s32[16,256]{1,0:T(8,128)}, u32[]{:S(2)}) copy-start(s32[16,256]{1,0:T(8,128)} %get-tuple-element.9) | copy-start | bytes 49156
  62.5 4.7 %copy-start.2 = (bf16[256,768]{1,0:T(8,128)(2,1)S(1)}, bf16[256,768]{1,0:T(8,128)(2,1)}, u32[]{:S(2)}) copy-start(bf16[256,768]{1,0:T(8,128)(2,1)} %win_ref.1) | copy-start | bytes 1179652
  62.5 34.3 %copy-start.4 = (f32[256,256]{1,0:T(8,128)S(1)}, f32[256,256]{1,0:T(8,128)}, u32[]{:S(2)}) copy-start(f32[256,256]{1,0:T(8,128)} %pos_ref.1) | copy-start | bytes 786436
  62.5 34.2 %copy-start.5 = (bf16[256,256]{1,0:T(8,128)(2,1)S(1)}, bf16[256,256]{1,0:T(8,128)(2,1)}, u32[]{:S(2)}) copy-start(bf16[256,256]{1,0:T(8,128)(2,1)} %wout_ref.1) | copy-start | bytes 393220
  62.5 34.2 %copy-start.6 = (f32[256]{0:T(256)S(1)}, f32[256]{0:T(256)}, u32[]{:S(2)}) copy-start(f32[256]{0:T(256)} %param.16) | copy-start | bytes 3076
  62.5 34.2 %copy-start.7 = (s32[16]{0:T(128)S(1)}, s32[16]{0:T(128)}, u32[]{:S(2)}) copy-start(s32[16]{0:T(128)} %lens_ref.1) | copy-start | bytes 196
  62.5 34.2 %all-to-all-start.1 = ((bf16[128,32,256]{2,1,0:T(8,128)(2,1)}), bf16[128,32,256]{2,1,0:T(8,128)(2,1)S(1)}, u32[]{:S(2)}, u32[]{:S(2)}) async-start(bf16[128,32,256]{2,1,0:T(8,128)(2,1)} %bitcast.4), calls=%async_computation.1 | async-start | bytes 4194304 | tf_op jit(solution)/shard_map/all_to_all | solution.py:361
  96.8 1.6 copy-start.1
  193.7 1.1 copy-start.8

commit v3 on v2

--- a/solution.py
+++ b/solution.py
@@ -275,7 +275,7 @@
 
 
 def graph_kernel(
-    tile_ref, part_ref, left_ref, own_ref, right_ref, held_ref, *refs
+    tile_ref, part_ref, left_ref, own_ref, right_ref, held_ref, swapped_ref, *refs
 ):
     arrived_refs = refs[: -5]
     wanted_ref, found_ref, table, weights_ref, sems = refs[-5:]
@@ -287,9 +287,14 @@
         (src, table.at[pl.ds(i * rows_item, rows_item)])
         for i, src in enumerate((left_ref, own_ref, right_ref))
     ]
-    moves.append((held_ref.at[pl.ds(part * row_tiles, row_tiles)], weights_ref.at[part]))
+    spot, side = part // 2, lax.rem(part, 2)
+    chips = groups // 2
+    moves.append((held_ref.at[spot, side], weights_ref.at[part]))
+    moves.append((swapped_ref.at[spot], weights_ref.at[2 * spot + 1 - side]))
     for k, src in enumerate(arrived_refs):
-        moves.append((src, weights_ref.at[lax.rem(part + groups - 1 - k, groups)]))
+        chip = lax.rem(spot + chips - 1 - k, chips)
+        moves.append((src.at[0], weights_ref.at[2 * chip + side]))
+        moves.append((src.at[1], weights_ref.at[2 * chip + 1 - side]))
     copies = [
         pltpu.make_async_copy(src, dst, sems.at[i]) for i, (src, dst) in enumerate(moves)
     ]
@@ -321,26 +326,26 @@
         found_ref[128 * b : 128 * b + 128, :] = dotf(pick, propagated).astype(jnp.bfloat16)
 
 
-def graph(tile_ids, part, left, own, right, held, arrived, wanted):
+def graph(tile_ids, part, left, own, right, held, swapped, arrived, wanted):
     rows_item, feat = own.shape
     count = wanted.shape[0] * wanted.shape[1]
     anywhere = pl.BlockSpec(memory_space=pl.ANY)
     scalars = pl.BlockSpec(memory_space=pltpu.SMEM)
     near = pl.BlockSpec(memory_space=pltpu.VMEM)
-    block = arrived[0].shape
+    groups = 2 * held.shape[0]
     return pl.pallas_call(
         graph_kernel,
         out_shape=jax.ShapeDtypeStruct((count, feat), jnp.bfloat16),
-        in_specs=[scalars, scalars] + [anywhere] * (4 + len(arrived)) + [near],
+        in_specs=[scalars, scalars] + [anywhere] * (5 + len(arrived)) + [near],
         out_specs=near,
         scratch_shapes=[
             pltpu.VMEM((3 * rows_item, feat), jnp.bfloat16),
-            pltpu.VMEM((1 + len(arrived),) + block, jnp.bfloat16),
-            pltpu.SemaphoreType.DMA((4 + len(arrived),)),
+            pltpu.VMEM((groups,) + held.shape[2:], jnp.bfloat16),
+            pltpu.SemaphoreType.DMA((3 + groups,)),
         ],
         compiler_params=pltpu.CompilerParams(vmem_limit_bytes=40 * 2**20),
         name="graph",
-    )(tile_ids, part, left, own, right, held, *arrived, wanted)
+    )(tile_ids, part, left, own, right, held, swapped, *arrived, wanted)
 
 
 def sum_kernel(parts_ref, out_ref):
@@ -379,13 +384,23 @@
     left = lax.ppermute(item_table, "item", [(i, (i + 1) % n_item) for i in range(n_item)])
     right = lax.ppermute(item_table, "item", [((i + 1) % n_item, i) for i in range(n_item)])
     mine = lax.axis_index("batch")
+    spot, side = mine // 2, lax.rem(mine, 2)
+    chips = n_batch // 2
+    by_owner = tile_weights.reshape(chips, 2, row_tiles, slots, tile, tile)
+    swapped = lax.ppermute(
+        lax.dynamic_index_in_dim(by_owner, 1 - side, 1, keepdims=False),
+        "batch",
+        [(i, i ^ 1) for i in range(n_batch)],
+    )
     arrived = []
-    for k in range(1, n_batch):
-        block = lax.dynamic_slice_in_dim(
-            tile_weights, lax.rem(mine + k, n_batch) * row_tiles, row_tiles, 0
-        )
+    for k in range(1, chips):
+        chip = lax.rem(spot + k, chips)
+        own_part = lax.dynamic_slice(
+            by_owner, (chip, side, 0, 0, 0, 0), (1, 1, row_tiles, slots, tile, tile)
+        )[0]
+        pair = jnp.concatenate([own_part, lax.dynamic_slice_in_dim(swapped, chip, 1, 0)], axis=0)
         arrived.append(
-            lax.ppermute(block, "batch", [(i, (i + k) % n_batch) for i in range(n_batch)])
+            lax.ppermute(pair, "batch", [(i, (i + 2 * k) % n_batch) for i in range(n_batch)])
         )
     sent, place = route(history, n_batch, n_item)
     per_peer = sent.shape[1]
@@ -398,7 +413,7 @@
     tile_ids = lax.dynamic_index_in_dim(
         got[:, per_peer:].reshape(n_batch, n_item, row_tiles * slots), here, 1, keepdims=False
     ).reshape(-1)
-    found = graph(tile_ids, mine.reshape(1), left, item_table, right, tile_weights, arrived, wanted)
+    found = graph(tile_ids, mine.reshape(1), left, item_table, right, by_owner, swapped, arrived, wanted)
     rows = exchange(found.reshape(peers, per_peer, feat), everyone).reshape(-1, feat)
     pack_rows = peers * 24
     block_out, packed = attention(

time: 195 us -> 184 us (0.944)
  waiting for transfers between devices: 58.9 us -> 43.7 us
  other arithmetic: 1.04 us -> 3.55 us
  blocking collectives: 45.8 us -> 48.2 us
  Pallas kernels: 56.9 us -> 54.9 us
    ppermute x7 -> x4, waiting for transfers between devices: 20 us -> 0.01 us  [the longest x3 0.01 us: local(): lax.ppermute(pair, 'batch', [(i, (i + 2 * k) % n_batch) for i in range(n_...]
    all_to_all x2, waiting for transfers between devices: 38.9 us -> 43.7 us  [exchange(): return lax.all_to_all(cells, axes, split_axis=0, concat_axis=0, tiled=True)]
    all_to_all x2, starting transfers between devices: 9.13 us -> 11.9 us  [exchange(): return lax.all_to_all(cells, axes, split_axis=0, concat_axis=0, tiled=True)]
    dynamic_slice x1, local copies, waits for them, and re-layouts: 2.73 us -> 0.06 us  [local(): lax.dynamic_slice_in_dim(swapped, chip, 1, 0)]
    squeeze x0 -> x2, local copies, waits for them, and re-layouts: none -> 2.51 us  [the longest x1 2.46 us: local(): lax.dynamic_index_in_dim(by_owner, 1 - side, 1, keepdims=False)]
    concatenate x0 -> x3, other arithmetic: none -> 2.51 us  [local(): jnp.concatenate([own_part, lax.dynamic_slice_in_dim(swapped, chip, 1, 0)]...]
    all_to_all x2, blocking collectives: 45.8 us -> 48.2 us  [exchange(): return lax.all_to_all(cells, axes, split_axis=0, concat_axis=0, tiled=True)]
    ppermute x7 -> x4, starting transfers between devices: 7.28 us -> 6.24 us  [the longest x3 4.81 us: local(): lax.ppermute(pair, 'batch', [(i, (i + 2 * k) % n_batch) for i in range(n_...]
  transfers between devices with their start and end apart: 11 -> 8, of which waited for: 6 -> 2; matrix products, arithmetic and copies ran while one was open for 3% -> 3% of each run, Pallas kernels for 1% -> 1%
where the time goes in v3:
time: 184 us
  Pallas kernels  54.9 us (30%)
  blocking collectives  48.2 us (26%)
  waiting for transfers between devices  43.7 us (24%)
  starting transfers between devices  24.4 us (13%)
  local copies, waits for them, and re-layouts  8.73 us (5%)
  other arithmetic  3.55 us (2%)
    all_to_all x2, blocking collectives, exchange(): return lax.all_to_all(cells, axes, split_axis=0, concat_axis=0, tiled=True)  48.2 us
    pallas_call x1, Pallas kernels, attention(): pl.pallas_call(attn_kernel, out_shape=(jax.ShapeDtypeStruct((users, lengt...  46.5 us
    all_to_all x2, waiting for transfers between devices, exchange(): return lax.all_to_all(cells, axes, split_axis=0, concat_axis=0, tiled=True)  43.7 us
    all_to_all x2, starting transfers between devices, exchange(): return lax.all_to_all(cells, axes, split_axis=0, concat_axis=0, tiled=True)  11.9 us
    pallas_call x1, Pallas kernels, graph(): pl.pallas_call(graph_kernel, out_shape=jax.ShapeDtypeStruct((count, feat)...  5.47 us
    ppermute x3, starting transfers between devices, local(): lax.ppermute(pair, 'batch', [(i, (i + 2 * k) % n_batch) for i in range(n_...  4.81 us
    ppermute x1, starting transfers between devices, local(): lax.ppermute(item_table, 'item', [((i + 1) % n_item, i) for i in range(n_...  4.57 us
  transfers between devices with their start and end apart: 8, of which 2 were waited for; matrix products, arithmetic and copies ran while one was open for 3% of the time, Pallas kernels for 1%

profile of v3, /device:TPU:1, one launch (start us, length us, event | category | flops | bytes accessed | tf_op | source)
XLA Modules:
  0.0 184.4 jit_solution(11151213164705044990)
XLA Ops:
  0.6 0.0 copy-start
  0.6 2.5 %dynamic-slice_bitcast_fusion = bf16[4,2,4,128,128]{4,3,2,1,0:T(8,128)(2,1)} fusion(bf16[4,2,2,4,128,128]{5,4,3,2,1,0:T(8,128)(2,1)} %bitcast.32, s32[]{:T(128)S(6)} %select_n.38), kind=kLoop, calls=%fused_computation | loop fusion | bytes 2097156 | tf_op jit(solution)/shard_map/jit(dynamic_index_in_dim)/squeeze | solution.py:391
  3.1 1.4 collective-permute-start.2
  4.5 1.7 collective-permute-start
  6.3 4.6 %collective-permute-start.1 = (bf16[2048,256]{1,0:T(8,128)(2,1)}, bf16[2048,256]{1,0:T(8,128)(2,1)}, u32[]{:S(2)}, u32[]{:S(2)}) collective-permute-start(bf16[2048,256]{1,0:T(8,128)(2,1)} %own_ref.1), channel_id=1, source_target_pairs={{1,0},{2,1},{3,2},{4,3},{5,4},{6,5},{7,6},{8,7},{9,8},{10,9},{11,1... | collective-permute-start | bytes 3145736 | tf_op jit(solution)/shard_map/ppermute | solution.py:385
  10.8 0.0 copy-done
  10.8 0.1 dynamic-slice_bitcast_fusion.1
  10.9 0.0 collective-permute-done.2.swapped_ref
  10.9 0.1 constant_dynamic-slice_fusion
  11.0 0.0 copy-start.10
  11.0 0.8 pad_maximum_fusion
  11.8 1.2 collective-permute-start.3
  13.0 0.8 pad_maximum_fusion.1
  13.9 2.5 %collective-permute-start.4 = (bf16[2,2,4,128,128]{4,3,2,1,0:T(8,128)(2,1)}, bf16[2,2,4,128,128]{4,3,2,1,0:T(8,128)(2,1)}, u32[]{:S(2)}, u32[]{:S(2)}) collective-permute-start(bf16[2,2,4,128,128]{4,3,2,1,0:T(8,128)(2,1)} %pad_maximum_fusion.1), channel_id=1, source_target_pairs={{0,64},{16,80},{32,96},{48,112},{64,0},{80,16},{96,32},{112,48},{1... | collective-permute-start | bytes 1572872 | tf_op jit(solution)/shard_map/ppermute | solution.py:403
  16.3 0.8 pad_maximum_fusion.2
  17.1 1.2 collective-permute-start.5
  18.3 2.7 %route.1 = (s32[128,32]{1,0:T(8,128)}, s32[16,256]{1,0:T(8,128)}) custom-call(s32[16,256]{1,0:T(8,128)} %hist_ref.1), custom_call_target="tpu_custom_call" | custom-call | tf_op jit(solution)/shard_map/route/pallas_call | solution.py:267
  21.0 0.0 copy-done.10
  21.0 0.1 copy.21
  21.1 0.1 broadcast_in_dim.7
  21.2 0.1 copy.22
  21.3 0.1 broadcast_in_dim.8
  21.3 0.1 reshape.55
  21.4 0.9 copy.23
  22.3 0.8 copy.24
  23.1 5.0 %all-to-all-start = ((s32[128,1,40]{2,1,0:T(1,128)}), s32[128,1,40]{2,1,0:T(1,128)S(1)}, u32[]{:S(2)}, u32[]{:S(2)}) async-start(s32[128,1,40]{2,1,0:T(1,128)} %bitcast), calls=%async_computation | async-start | bytes 131072 | tf_op jit(solution)/shard_map/all_to_all | solution.py:366
  28.1 14.4 %all-to-all-done = s32[128,1,40]{2,1,0:T(1,128)S(1)} async-done(((s32[128,1,40]{2,1,0:T(1,128)}), s32[128,1,40]{2,1,0:T(1,128)S(1)}, u32[]{:S(2)}, u32[]{:S(2)}) %all-to-all-start) | async-done | bytes 20512 | tf_op jit(solution)/shard_map/all_to_all | solution.py:366
  42.4 0.1 slice.52
  42.5 0.1 reshape.57.tile_ref
  42.6 0.1 reshape.60.refs_3_
  42.7 0.0 collective-permute-done.left_ref
  42.7 0.0 collective-permute-done.1.right_ref
  42.7 0.0 collective-permute-done.3.refs_0_
  42.7 0.0 collective-permute-done.4.refs_1_
  42.7 0.0 collective-permute-done.5.refs_2_
  42.7 0.0 copy-start.3
  42.8 1.2 copy-done.3
  44.0 5.5 %graph.1 = bf16[4096,256]{1,0:T(8,128)(2,1)} custom-call(s32[64]{0:T(128)S(1)} %reshape.57.tile_ref, s32[1]{0:T(128)} %bitcast.3.part_ref, bf16[2048,256]{1,0:T(8,128)(2,1)} %collective-permute-done.left_ref, bf16[2048,256]{1,0:T(8,128)(2,1)S(1)} %copy-done.3, bf16[2048,256]{1,0:T(8,128)(2,1)} %collective-permute-done.1.right_ref, ...), custom_call_target="tpu_custom_call" | custom-call | tf_op jit(solution)/shard_map/graph/pallas_call | solution.py:336
  49.5 0.0 copy-start.9
  49.5 0.0 copy-start.2
  49.5 0.0 copy-start.4
  49.5 0.0 copy-start.5
  49.5 0.0 copy-start.6
  49.5 0.0 copy-start.7
  49.5 6.9 %all-to-all-start.1 = ((bf16[128,32,256]{2,1,0:T(8,128)(2,1)}), bf16[128,32,256]{2,1,0:T(8,128)(2,1)S(1)}, u32[]{:S(2)}, u32[]{:S(2)}) async-start(bf16[128,32,256]{2,1,0:T(8,128)(2,1)} %bitcast.9), calls=%async_computation.1 | async-start | bytes 4194304 | tf_op jit(solution)/shard_map/all_to_all | solution.py:366
  56.4 0.0 copy-done.9
  56.4 0.0 copy-done.2
  56.4 0.2 copy.26
  56.6 29.3 %all-to-all-done.1 = bf16[128,32,256]{2,1,0:T(8,128)(2,1)S(1)} async-done(((bf16[128,32,256]{2,1,0:T(8,128)(2,1)}), bf16[128,32,256]{2,1,0:T(8,128)(2,1)S(1)}, u32[]{:S(2)}, u32[]{:S(2)}) %all-to-all-start.1) | async-done | bytes 2097184 | tf_op jit(solution)/shard_map/all_to_all | solution.py:366
  85.9 0.0 copy-done.4
  85.9 0.0 copy-done.5
  85.9 0.0 copy-done.6
  85.9 0.0 copy-done.7
  85.9 0.0 copy-start.1
  85.9 1.6 copy-done.1
  87.5 46.5 %attention.1 = (bf16[16,256,256]{2,1,0:T(8,128)(2,1)}, bf16[3072,128]{1,0:T(8,128)(2,1)S(1)}) custom-call(s32[16]{0:T(128)S(1)} %copy-done.7, s32[4096]{0:T(1024)S(1)} %bitcast.37, bf16[4096,256]{1,0:T(8,128)(2,1)S(1)} %bitcast.31, bf16[16,256,256]{2,1,0:T(8,128)(2,1)S(1)} %copy-done.1, f32[256,256]{1,0:T(8,128)S(1)} %copy-done.4, f32[1,256]{1,0:T(1,128)S(1)} %bitcast.38, ...), custom_call_target="tpu_custom_call" | custom-call | tf_op jit(solution)/shard_map/attention/pallas_call | solution.py:206
  134.1 27.8 %all_to_all.27.parts_ref = bf16[128,24,128]{2,1,0:T(8,128)(2,1)S(1)} all-to-all(bf16[128,24,128]{2,1,0:T(8,128)(2,1)S(1)} %bitcast.36), channel_id=1, replica_groups=mesh['batch'=8,'item'=16] {'batch','item'}, dimensions={0} | all-to-all | bytes 1572864 | tf_op jit(solution)/shard_map/all_to_all | solution.py:366
  161.9 0.2 sum_spread.1
  162.1 20.4 %all_to_all.28 = bf16[128,24,128]{2,1,0:T(8,128)(2,1)S(1)} all-to-all(bf16[128,24,128]{2,1,0:T(8,128)(2,1)S(1)} %sum_spread.1), channel_id=1, replica_groups=mesh['batch'=8,'item'=16] {'batch','item'}, dimensions={0} | all-to-all | bytes 1572864 | tf_op jit(solution)/shard_map/all_to_all | solution.py:366
  182.4 0.2 bitcast_convert_fusion
  182.6 0.6 slice_bitcast_fusion
  183.3 0.0 copy-start.8
  183.3 0.9 pad_maximum_fusion.3
  184.2 0.2 copy-done.8
  (10 shorter events, 0.1 us)
Async XLA Ops:
  0.6 10.2 %copy-start = (bf16[16,4,128,128]{3,2,1,0:T(8,128)(2,1)S(1)}, bf16[16,4,128,128]{3,2,1,0:T(8,128)(2,1)}, u32[]{:S(2)}) copy-start(bf16[16,4,128,128]{3,2,1,0:T(8,128)(2,1)} %param.12) | copy-start | bytes 6291460
  3.1 7.8 %collective-permute-start.2 = (bf16[4,2,4,128,128]{4,3,2,1,0:T(8,128)(2,1)}, bf16[4,2,4,128,128]{4,3,2,1,0:T(8,128)(2,1)S(1)}, u32[]{:S(2)}, u32[]{:S(2)}) collective-permute-start(bf16[4,2,4,128,128]{4,3,2,1,0:T(8,128)(2,1)} %dynamic-slice_bitcast_fusion), channel_id=1, source_target_pairs={{0,16},{16,0},{32,48},{48,32},{64,80},{80,64},{96,112},{112,96},{1... | collective-permute-start | bytes 3145736 | tf_op jit(solution)/shard_map/ppermute | solution.py:390
  4.5 38.2 %collective-permute-start = (bf16[2048,256]{1,0:T(8,128)(2,1)}, bf16[2048,256]{1,0:T(8,128)(2,1)}, u32[]{:S(2)}, u32[]{:S(2)}) collective-permute-start(bf16[2048,256]{1,0:T(8,128)(2,1)} %own_ref.1), channel_id=1, source_target_pairs={{0,1},{1,2},{2,3},{3,4},{4,5},{5,6},{6,7},{7,8},{8,9},{9,10},{10,1... | collective-permute-start | bytes 3145736 | tf_op jit(solution)/shard_map/ppermute | solution.py:384
  6.3 36.5 %collective-permute-start.1 = (bf16[2048,256]{1,0:T(8,128)(2,1)}, bf16[2048,256]{1,0:T(8,128)(2,1)}, u32[]{:S(2)}, u32[]{:S(2)}) collective-permute-start(bf16[2048,256]{1,0:T(8,128)(2,1)} %own_ref.1), channel_id=1, source_target_pairs={{1,0},{2,1},{3,2},{4,3},{5,4},{6,5},{7,6},{8,7},{9,8},{10,9},{11,1... | collective-permute-start | bytes 3145736 | tf_op jit(solution)/shard_map/ppermute | solution.py:385
  11.0 10.1 %copy-start.10 = (s32[16,4]{0,1:T(4,128)S(1)}, s32[16,4]{0,1:T(4,128)}, u32[]{:S(2)}) copy-start(s32[16,4]{0,1:T(4,128)} %param.11) | copy-start | bytes 772
  11.8 30.9 %collective-permute-start.3 = (bf16[2,2,4,128,128]{4,3,2,1,0:T(8,128)(2,1)}, bf16[2,2,4,128,128]{4,3,2,1,0:T(8,128)(2,1)}, u32[]{:S(2)}, u32[]{:S(2)}) collective-permute-start(bf16[2,2,4,128,128]{4,3,2,1,0:T(8,128)(2,1)} %pad_maximum_fusion), channel_id=1, source_target_pairs={{0,32},{16,48},{32,64},{48,80},{64,96},{80,112},{96,0},{112,16},{1... | collective-permute-start | bytes 1572872 | tf_op jit(solution)/shard_map/ppermute | solution.py:403
  13.9 28.9 %collective-permute-start.4 = (bf16[2,2,4,128,128]{4,3,2,1,0:T(8,128)(2,1)}, bf16[2,2,4,128,128]{4,3,2,1,0:T(8,128)(2,1)}, u32[]{:S(2)}, u32[]{:S(2)}) collective-permute-start(bf16[2,2,4,128,128]{4,3,2,1,0:T(8,128)(2,1)} %pad_maximum_fusion.1), channel_id=1, source_target_pairs={{0,64},{16,80},{32,96},{48,112},{64,0},{80,16},{96,32},{112,48},{1... | collective-permute-start | bytes 1572872 | tf_op jit(solution)/shard_map/ppermute | solution.py:403
  17.1 25.6 %collective-permute-start.5 = (bf16[2,2,4,128,128]{4,3,2,1,0:T(8,128)(2,1)}, bf16[2,2,4,128,128]{4,3,2,1,0:T(8,128)(2,1)}, u32[]{:S(2)}, u32[]{:S(2)}) collective-permute-start(bf16[2,2,4,128,128]{4,3,2,1,0:T(8,128)(2,1)} %pad_maximum_fusion.2), channel_id=1, source_target_pairs={{0,96},{16,112},{32,0},{48,16},{64,32},{80,48},{96,64},{112,80},{1... | collective-permute-start | bytes 1572872 | tf_op jit(solution)/shard_map/ppermute | solution.py:403
  23.1 19.4 %all-to-all-start = ((s32[128,1,40]{2,1,0:T(1,128)}), s32[128,1,40]{2,1,0:T(1,128)S(1)}, u32[]{:S(2)}, u32[]{:S(2)}) async-start(s32[128,1,40]{2,1,0:T(1,128)} %bitcast), calls=%async_computation | async-start | bytes 131072 | tf_op jit(solution)/shard_map/all_to_all | solution.py:366
  42.7 1.2 copy-start.3
  49.5 7.0 %copy-start.9 = (s32[16,256]{1,0:T(8,128)S(1)}, s32[16,256]{1,0:T(8,128)}, u32[]{:S(2)}) copy-start(s32[16,256]{1,0:T(8,128)} %get-tuple-element.9) | copy-start | bytes 49156
  49.5 7.0 %copy-start.2 = (bf16[256,768]{1,0:T(8,128)(2,1)S(1)}, bf16[256,768]{1,0:T(8,128)(2,1)}, u32[]{:S(2)}) copy-start(bf16[256,768]{1,0:T(8,128)(2,1)} %win_ref.1) | copy-start | bytes 1179652
  49.5 36.4 %copy-start.4 = (f32[256,256]{1,0:T(8,128)S(1)}, f32[256,256]{1,0:T(8,128)}, u32[]{:S(2)}) copy-start(f32[256,256]{1,0:T(8,128)} %pos_ref.1) | copy-start | bytes 786436
  49.5 36.4 %copy-start.5 = (bf16[256,256]{1,0:T(8,128)(2,1)S(1)}, bf16[256,256]{1,0:T(8,128)(2,1)}, u32[]{:S(2)}) copy-start(bf16[256,256]{1,0:T(8,128)(2,1)} %wout_ref.1) | copy-start | bytes 393220
  49.5 36.4 %copy-start.6 = (f32[256]{0:T(256)S(1)}, f32[256]{0:T(256)}, u32[]{:S(2)}) copy-start(f32[256]{0:T(256)} %param.16) | copy-start | bytes 3076
  49.5 36.4 %copy-start.7 = (s32[16]{0:T(128)S(1)}, s32[16]{0:T(128)}, u32[]{:S(2)}) copy-start(s32[16]{0:T(128)} %lens_ref.1) | copy-start | bytes 196
  49.5 36.4 %all-to-all-start.1 = ((bf16[128,32,256]{2,1,0:T(8,128)(2,1)}), bf16[128,32,256]{2,1,0:T(8,128)(2,1)S(1)}, u32[]{:S(2)}, u32[]{:S(2)}) async-start(bf16[128,32,256]{2,1,0:T(8,128)(2,1)} %bitcast.9), calls=%async_computation.1 | async-start | bytes 4194304 | tf_op jit(solution)/shard_map/all_to_all | solution.py:366
  85.9 1.6 copy-start.1
  183.3 1.1 copy-start.8

commit v4 on v3

--- a/solution.py
+++ b/solution.py
@@ -29,33 +29,38 @@
     )
 
 
-def user_pass(
-    n, live_len, x_ref, bring, cot_ref, pos_ref, gain_ref, win_ref, wint_ref, wout_ref,
+def pair_pass(
+    extents, lives, x_ref, bring, cot_ref, pos_ref, gain_ref, win_ref, wint_ref, wout_ref,
     blk_ref, gin_ref, gout_ref, ggain_ref, gpos_ref, gkt_ref, gvt_ref, mxt_ref, gqt_ref, bias_ref,
 ):
     feat = pos_ref.shape[1]
     hd = feat // HEADS
     scale = hd ** (-0.5)
     bf = jnp.bfloat16
-    resid = jnp.concatenate([x_ref[:n, 0, :], x_ref[:n, 1, :]], axis=1) + pos_ref[:n, :]
-    inv = lax.rsqrt(jnp.mean(resid * resid, axis=1, keepdims=True) + 1e-05)
     gain = gain_ref[...]
-    rnorm = resid * inv
-    normed = (rnorm * gain).astype(bf)
-    kv = dotf(normed, win_ref[:, feat:]).astype(bf)
-    qkvt = dotf(wint_ref[...], normed, NT).astype(bf)
-    live = lax.broadcasted_iota(jnp.int32, (n, feat), 0) < live_len
-    gres = jnp.where(live, cot_ref[0, :n, :].astype(jnp.float32), 0.0)
-    glow = gres.astype(bf)
-    gmt = dotf(wout_ref[...], glow, NT).astype(bf)
-    fill = jnp.zeros((2 * hd, 2 * BLK), bf)
-    items = [(ib, pair) for ib in range(n // BLK) for pair in range(HEADS // 2)]
-
-    def products(ib, pair):
+    state = {}
+
+    def head(w):
+        n = extents[w]
+        resid = jnp.concatenate([x_ref[w, :n, 0, :], x_ref[w, :n, 1, :]], axis=1) + pos_ref[:n, :]
+        inv = lax.rsqrt(jnp.mean(resid * resid, axis=1, keepdims=True) + 1e-05)
+        rnorm = resid * inv
+        normed = (rnorm * gain).astype(bf)
+        kv = dotf(normed, win_ref[:, feat:]).astype(bf)
+        qkvt = dotf(wint_ref[...], normed, NT).astype(bf)
+        live = lax.broadcasted_iota(jnp.int32, (n, feat), 0) < lives[w]
+        gres = jnp.where(live, cot_ref[w, :n, :].astype(jnp.float32), 0.0)
+        glow = gres.astype(bf)
+        gmt = dotf(wout_ref[...], glow, NT).astype(bf)
+        state[w] = (resid, inv, rnorm, normed, kv, qkvt, live, gres, glow, gmt)
+
+    def products(w, ib, pair):
+        kv, qkvt, gmt = state[w][4], state[w][5], state[w][9]
         r0 = 2 * hd * pair
         quad = 128 * (r0 // 128)
         i0 = ib * BLK
         nj = i0 + BLK
+        fill = jnp.zeros((2 * hd, 2 * BLK), bf)
         qd = diag2(qkvt[r0 : r0 + hd, i0:nj], qkvt[r0 + hd : r0 + 2 * hd, i0:nj])
         md = diag2(gmt[r0 : r0 + hd, i0:nj], gmt[r0 + hd : r0 + 2 * hd, i0:nj])
         widen = lambda d: jnp.concatenate([d, fill] if r0 == quad else [fill, d], axis=0)
@@ -63,7 +68,7 @@
         gp = dotf(kv[:nj, feat + quad : feat + quad + 128], widen(md))
         return qd, md, sc, gp
 
-    def soften(ib, pair, made):
+    def soften(w, ib, pair, made):
         qd, md, sc, gp = made
         i0 = ib * BLK
         edge = sc[i0:] + bias_ref[...]
@@ -76,7 +81,9 @@
         gs = (prob * (gp - inner)).astype(bf)
         return qd, md, plow, gs
 
-    def collect(ib, pair, made):
+    def collect(w, ib, pair, made):
+        n = extents[w]
+        qkvt = state[w][5]
         qd, md, plow, gs = made
         r0 = 2 * hd * pair
         i0 = ib * BLK
@@ -87,43 +94,60 @@
         gq = dotf(kt, gs)
         gk = dotf(qd, gs, NT) * scale
         gv = dotf(md, plow, NT)
-        mxt_ref[r0 : r0 + hd, i0:nj] = mt[:hd, :BLK].astype(bf)
-        mxt_ref[r0 + hd : r0 + 2 * hd, i0:nj] = mt[hd:, BLK:].astype(bf)
-        gqt_ref[r0 : r0 + hd, i0:nj] = (gq[:hd, :BLK] * scale).astype(bf)
-        gqt_ref[r0 + hd : r0 + 2 * hd, i0:nj] = (gq[hd:, BLK:] * scale).astype(bf)
+        mxt_ref[w, r0 : r0 + hd, i0:nj] = mt[:hd, :BLK].astype(bf)
+        mxt_ref[w, r0 + hd : r0 + 2 * hd, i0:nj] = mt[hd:, BLK:].astype(bf)
+        gqt_ref[w, r0 : r0 + hd, i0:nj] = (gq[:hd, :BLK] * scale).astype(bf)
+        gqt_ref[w, r0 + hd : r0 + 2 * hd, i0:nj] = (gq[hd:, BLK:] * scale).astype(bf)
         if n > BLK and ib == 0:
-            gkt_ref[r0 : r0 + 2 * hd, :] = gk
-            gvt_ref[r0 : r0 + 2 * hd, :] = gv
+            gkt_ref[w, r0 : r0 + 2 * hd, :] = gk
+            gvt_ref[w, r0 : r0 + 2 * hd, :] = gv
         else:
             if ib > 0:
-                gk = jnp.concatenate([gk[:, :BLK] + gkt_ref[r0 : r0 + 2 * hd, :], gk[:, BLK:]], axis=1)
-                gv = jnp.concatenate([gv[:, :BLK] + gvt_ref[r0 : r0 + 2 * hd, :], gv[:, BLK:]], axis=1)
-            gqt_ref[feat + r0 : feat + r0 + 2 * hd, :n] = gk.astype(bf)
-            gqt_ref[2 * feat + r0 : 2 * feat + r0 + 2 * hd, :n] = gv.astype(bf)
-
+                gk = jnp.concatenate([gk[:, :BLK] + gkt_ref[w, r0 : r0 + 2 * hd, :], gk[:, BLK:]], axis=1)
+                gv = jnp.concatenate([gv[:, :BLK] + gvt_ref[w, r0 : r0 + 2 * hd, :], gv[:, BLK:]], axis=1)
+            gqt_ref[w, feat + r0 : feat + r0 + 2 * hd, :n] = gk.astype(bf)
+            gqt_ref[w, 2 * feat + r0 : 2 * feat + r0 + 2 * hd, :n] = gv.astype(bf)
+
+    def tail(w):
+        n = extents[w]
+        resid, inv, rnorm, normed, kv, qkvt, live, gres, glow, gmt = state[w]
+        mxt = mxt_ref[w, :, :n]
+        attn = dotf(mxt, wout_ref[...], TN)
+        blk_ref[w, :n, :] = jnp.where(live, resid + attn, 0.0).astype(bf)
+        if n < blk_ref.shape[1]:
+            blk_ref[w, n:, :] = jnp.zeros((blk_ref.shape[1] - n, feat), bf)
+        gout_ref[...] += dotf(mxt, glow)
+        gqkvt = gqt_ref[w, :, :n]
+        gin_ref[...] += dotf(gqkvt, normed)
+        gn = dotf(win_ref[...], gqkvt).T
+        scaled = gn * gain
+        ggain_ref[...] += jnp.sum(gn * rnorm, axis=0, keepdims=True)
+        corr = jnp.mean(scaled * resid, axis=1, keepdims=True) * (inv * inv * inv)
+        gpos_ref[:n, :] += gres + inv * scaled - resid * corr
+
+    items = [
+        (w, ib, pair)
+        for w in range(len(extents))
+        for ib in range(extents[w] // BLK)
+        for pair in range(HEADS // 2)
+    ]
+    first = len([i for i in items if i[0] == 0])
     made, soft = {}, {}
+    head(0)
     for t in range(len(items) + 2):
         if t < len(items):
             bring(t, len(items))
+            if t == 3:
+                head(1)
             made[t] = products(*items[t])
         if t >= 2:
             collect(*items[t - 2], soft.pop(t - 2))
+        if t - 2 == first - 1 + 2:
+            tail(0)
         s = t - 1
         if 0 <= s < len(items):
             soft[s] = soften(*items[s], made.pop(s))
-    mxt = mxt_ref[:, :n]
-    attn = dotf(mxt, wout_ref[...], TN)
-    blk_ref[0, :n, :] = jnp.where(live, resid + attn, 0.0).astype(bf)
-    if n < blk_ref.shape[1]:
-        blk_ref[0, n:, :] = jnp.zeros((blk_ref.shape[1] - n, feat), bf)
-    gout_ref[...] += dotf(mxt, glow)
-    gqkvt = gqt_ref[:, :n]
-    gin_ref[...] += dotf(gqkvt, normed)
-    gn = dotf(win_ref[...], gqkvt).T
-    scaled = gn * gain
-    ggain_ref[...] += jnp.sum(gn * rnorm, axis=0, keepdims=True)
-    corr = jnp.mean(scaled * resid, axis=1, keepdims=True) * (inv * inv * inv)
-    gpos_ref[:n, :] += gres + inv * scaled - resid * corr
+    tail(1)
 
 
 def attn_kernel(
@@ -133,15 +157,15 @@
 ):
     users, length, feat = cot_ref.shape
 
-    def bring(user, first, count):
+    def bring(pair, first, count):
         for t in range(first, first + count, 16):
-            some = [rowf_ref[idx_ref[user * length + t + k]] for k in range(16)]
+            some = [rowf_ref[idx_ref[pair * 2 * length + t + k]] for k in range(16)]
             for k in range(16):
-                x_ref[user % 2, t + k] = some[k]
+                x_ref[pair % 2, (t + k) // length, (t + k) % length] = some[k]
 
     rowf_ref[:, 0, :] = rows_ref[:, :128].astype(jnp.float32)
     rowf_ref[:, 1, :] = rows_ref[:, 128:].astype(jnp.float32)
-    bring(0, 0, length)
+    bring(0, 0, 2 * length)
     gin_ref[...] = jnp.zeros_like(gin_ref)
     gout_ref[...] = jnp.zeros_like(gout_ref)
     ggain_ref[...] = jnp.zeros_like(ggain_ref)
@@ -150,38 +174,43 @@
     row = lax.broadcasted_iota(jnp.int32, (BLK, 2 * BLK), 0)
     bias_ref[...] = jnp.where(row <= (lane & (BLK - 1)), 0.0, -1e30)
 
-    def put(u):
-        return pltpu.make_async_copy(held_ref.at[u % 2], out_ref.at[u], sems.at[u % 2])
-
-    def step(u, carry):
-        live_len = lens_ref[u]
-        coming = jnp.minimum(u + 1, users - 1)
-
-        @pl.when(u >= 2)
+    def put(p):
+        return pltpu.make_async_copy(
+            held_ref.at[p % 2], out_ref.at[pl.ds(2 * p, 2)], sems.at[p % 2]
+        )
+
+    pairs = users // 2
+
+    def step(p, carry):
+        lives = (lens_ref[2 * p], lens_ref[2 * p + 1])
+        coming = jnp.minimum(p + 1, pairs - 1)
+
+        @pl.when(p >= 2)
         def _():
-            put(u - 2).wait()
-
-        def run(n):
-            user_pass(
-                n, live_len, x_ref.at[u % 2],
-                lambda t, of: bring(coming, t * length // of, length // of),
-                cot_ref.at[pl.ds(u, 1)], pos_ref, gain_ref, win_ref, wint_ref, wout_ref,
-                held_ref.at[pl.ds(u % 2, 1)], gin_ref, gout_ref, ggain_ref, gpos_ref,
+            put(p - 2).wait()
+
+        def run(extents):
+            def fetch(t, of):
+                part = [16 * (2 * length // 16 * i // of) for i in (t, t + 1)]
+                bring(coming, part[0], part[1] - part[0])
+
+            pair_pass(
+                extents, lives, x_ref.at[p % 2], fetch,
+                cot_ref.at[pl.ds(2 * p, 2)], pos_ref, gain_ref, win_ref, wint_ref, wout_ref,
+                held_ref.at[p % 2], gin_ref, gout_ref, ggain_ref, gpos_ref,
                 gkt_ref, gvt_ref, mxt_ref, gqt_ref, bias_ref,
             )
 
-        @pl.when(live_len <= BLK)
-        def _():
-            run(BLK)
-
-        @pl.when(live_len > BLK)
-        def _():
-            run(length)
-
-        put(u).start()
+        for a in (BLK, length):
+            for b in (BLK, length):
+                fits = (lives[0] <= BLK) == (a == BLK)
+                fits &= (lives[1] <= BLK) == (b == BLK)
+                pl.when(fits)(functools.partial(run, (a, b)))
+
+        put(p).start()
         return carry
 
-    lax.fori_loop(0, users, step, 0)
+    lax.fori_loop(0, pairs, step, 0)
     gin = gin_ref[...].T
     at = 0
     for whole in (gin, gout_ref[...], gpos_ref[...]):
@@ -194,8 +223,8 @@
     gg = ggain_ref[...]
     both = jnp.where(top_row == 0, gg[:, :128], jnp.where(top_row == 1, gg[:, 128:], 0.0))
     pack_ref[at : at + 16, :] = both.astype(pack_ref.dtype)
-    put(users - 2).wait()
-    put(users - 1).wait()
+    put(pairs - 2).wait()
+    put(pairs - 1).wait()
 
 
 def attention(rows, idx, lengths, cot, position, gain, win, wint, wout, pack_rows, pack_type):
@@ -213,17 +242,17 @@
         out_specs=(pl.BlockSpec(memory_space=pl.ANY), near),
         scratch_shapes=[
             pltpu.VMEM((rows.shape[0], 2, 128), f32),
-            pltpu.VMEM((2, length, 2, 128), f32),
-            pltpu.VMEM((feat, BLK), f32),
-            pltpu.VMEM((feat, BLK), f32),
-            pltpu.VMEM((feat, length), bf),
-            pltpu.VMEM((3 * feat, length), bf),
+            pltpu.VMEM((2, 2, length, 2, 128), f32),
+            pltpu.VMEM((2, feat, BLK), f32),
+            pltpu.VMEM((2, feat, BLK), f32),
+            pltpu.VMEM((2, feat, length), bf),
+            pltpu.VMEM((2, 3 * feat, length), bf),
             pltpu.VMEM((3 * feat, feat), f32),
             pltpu.VMEM((feat, feat), f32),
             pltpu.VMEM((1, feat), f32),
             pltpu.VMEM((length, feat), f32),
             pltpu.VMEM((BLK, 2 * BLK), f32),
-            pltpu.VMEM((2, length, feat), bf),
+            pltpu.VMEM((2, 2, length, feat), bf),
             pltpu.SemaphoreType.DMA((2,)),
         ],
         compiler_params=pltpu.CompilerParams(vmem_limit_bytes=40 * 2**20),

time: 184 us -> 181 us (0.984)
  blocking collectives: 48.2 us -> 41.4 us
  Pallas kernels: 54.9 us -> 57.8 us
    all_to_all x2, blocking collectives: 48.2 us -> 41.4 us  [exchange(): return lax.all_to_all(cells, axes, split_axis=0, concat_axis=0, tiled=True)]
    pallas_call x1, Pallas kernels: 46.5 us -> 49.5 us  [attention(): pl.pallas_call(attn_kernel, out_shape=(jax.ShapeDtypeStruct((users, lengt...]
  transfers between devices with their start and end apart: 8 -> 8, of which waited for: 2 -> 2; matrix products, arithmetic and copies ran while one was open for 3% -> 3% of each run, Pallas kernels for 1% -> 2%
where the time goes in v4:
time: 181 us; the launch traced here: 180 us
  Pallas kernels  57.8 us (32%)
  waiting for transfers between devices  43.7 us (24%)
  blocking collectives  41.4 us (23%)
  starting transfers between devices  24.4 us (13%)
  local copies, waits for them, and re-layouts  8.73 us (5%)
  other arithmetic  3.55 us (2%)
    pallas_call x1, Pallas kernels, attention(): pl.pallas_call(attn_kernel, out_shape=(jax.ShapeDtypeStruct((users, lengt...  49.5 us
    all_to_all x2, waiting for transfers between devices, exchange(): return lax.all_to_all(cells, axes, split_axis=0, concat_axis=0, tiled=True)  43.7 us
    all_to_all x2, blocking collectives, exchange(): return lax.all_to_all(cells, axes, split_axis=0, concat_axis=0, tiled=True)  41.4 us
    all_to_all x2, starting transfers between devices, exchange(): return lax.all_to_all(cells, axes, split_axis=0, concat_axis=0, tiled=True)  11.8 us
    pallas_call x1, Pallas kernels, graph(): pl.pallas_call(graph_kernel, out_shape=jax.ShapeDtypeStruct((count, feat)...  5.47 us
    ppermute x3, starting transfers between devices, local(): lax.ppermute(pair, 'batch', [(i, (i + 2 * k) % n_batch) for i in range(n_...  4.81 us
    ppermute x1, starting transfers between devices, local(): lax.ppermute(item_table, 'item', [((i + 1) % n_item, i) for i in range(n_...  4.57 us
  transfers between devices with their start and end apart: 8, of which 2 were waited for; matrix products, arithmetic and copies ran while one was open for 3% of the time, Pallas kernels for 2%

profile of v4, /device:TPU:1, one launch (start us, length us, event | category | flops | bytes accessed | tf_op | source)
XLA Modules:
  0.0 180.5 jit_solution(1171863907860656018)
XLA Ops:
  0.6 0.0 copy-start
  0.6 2.5 %dynamic-slice_bitcast_fusion = bf16[4,2,4,128,128]{4,3,2,1,0:T(8,128)(2,1)} fusion(bf16[4,2,2,4,128,128]{5,4,3,2,1,0:T(8,128)(2,1)} %bitcast.32, s32[]{:T(128)S(6)} %select_n.38), kind=kLoop, calls=%fused_computation | loop fusion | bytes 2097156 | tf_op jit(solution)/shard_map/jit(dynamic_index_in_dim)/squeeze | solution.py:420
  3.1 1.4 collective-permute-start.2
  4.5 1.7 collective-permute-start
  6.3 4.6 %collective-permute-start.1 = (bf16[2048,256]{1,0:T(8,128)(2,1)}, bf16[2048,256]{1,0:T(8,128)(2,1)}, u32[]{:S(2)}, u32[]{:S(2)}) collective-permute-start(bf16[2048,256]{1,0:T(8,128)(2,1)} %own_ref.1), channel_id=1, source_target_pairs={{1,0},{2,1},{3,2},{4,3},{5,4},{6,5},{7,6},{8,7},{9,8},{10,9},{11,1... | collective-permute-start | bytes 3145736 | tf_op jit(solution)/shard_map/ppermute | solution.py:414
  10.8 0.0 copy-done
  10.8 0.1 dynamic-slice_bitcast_fusion.1
  10.9 0.0 collective-permute-done.2.swapped_ref
  10.9 0.1 constant_dynamic-slice_fusion
  11.0 0.0 copy-start.10
  11.0 0.8 pad_maximum_fusion
  11.8 1.2 collective-permute-start.3
  13.0 0.8 pad_maximum_fusion.1
  13.9 2.5 %collective-permute-start.4 = (bf16[2,2,4,128,128]{4,3,2,1,0:T(8,128)(2,1)}, bf16[2,2,4,128,128]{4,3,2,1,0:T(8,128)(2,1)}, u32[]{:S(2)}, u32[]{:S(2)}) collective-permute-start(bf16[2,2,4,128,128]{4,3,2,1,0:T(8,128)(2,1)} %pad_maximum_fusion.1), channel_id=1, source_target_pairs={{0,64},{16,80},{32,96},{48,112},{64,0},{80,16},{96,32},{112,48},{1... | collective-permute-start | bytes 1572872 | tf_op jit(solution)/shard_map/ppermute | solution.py:432
  16.3 0.8 pad_maximum_fusion.2
  17.1 1.2 collective-permute-start.5
  18.3 2.7 %route.1 = (s32[128,32]{1,0:T(8,128)}, s32[16,256]{1,0:T(8,128)}) custom-call(s32[16,256]{1,0:T(8,128)} %hist_ref.1), custom_call_target="tpu_custom_call" | custom-call | tf_op jit(solution)/shard_map/route/pallas_call | solution.py:296
  21.0 0.0 copy-done.10
  21.0 0.1 copy.21
  21.1 0.1 broadcast_in_dim.7
  21.2 0.1 copy.22
  21.3 0.1 broadcast_in_dim.8
  21.3 0.1 reshape.55
  21.4 0.9 copy.23
  22.3 0.8 copy.24
  23.1 5.0 %all-to-all-start = ((s32[128,1,40]{2,1,0:T(1,128)}), s32[128,1,40]{2,1,0:T(1,128)S(1)}, u32[]{:S(2)}, u32[]{:S(2)}) async-start(s32[128,1,40]{2,1,0:T(1,128)} %bitcast), calls=%async_computation | async-start | bytes 131072 | tf_op jit(solution)/shard_map/all_to_all | solution.py:395
  28.1 14.4 %all-to-all-done = s32[128,1,40]{2,1,0:T(1,128)S(1)} async-done(((s32[128,1,40]{2,1,0:T(1,128)}), s32[128,1,40]{2,1,0:T(1,128)S(1)}, u32[]{:S(2)}, u32[]{:S(2)}) %all-to-all-start) | async-done | bytes 20512 | tf_op jit(solution)/shard_map/all_to_all | solution.py:395
  42.4 0.1 slice.52
  42.5 0.1 reshape.57.tile_ref
  42.6 0.1 reshape.60.refs_3_
  42.7 0.0 collective-permute-done.left_ref
  42.7 0.0 collective-permute-done.1.right_ref
  42.7 0.0 collective-permute-done.3.refs_0_
  42.7 0.0 collective-permute-done.4.refs_1_
  42.7 0.0 collective-permute-done.5.refs_2_
  42.7 0.0 copy-start.3
  42.8 1.2 copy-done.3
  44.0 5.5 %graph.1 = bf16[4096,256]{1,0:T(8,128)(2,1)} custom-call(s32[64]{0:T(128)S(1)} %reshape.57.tile_ref, s32[1]{0:T(128)} %bitcast.3.part_ref, bf16[2048,256]{1,0:T(8,128)(2,1)} %collective-permute-done.left_ref, bf16[2048,256]{1,0:T(8,128)(2,1)S(1)} %copy-done.3, bf16[2048,256]{1,0:T(8,128)(2,1)} %collective-permute-done.1.right_ref, ...), custom_call_target="tpu_custom_call" | custom-call | tf_op jit(solution)/shard_map/graph/pallas_call | solution.py:365
  49.5 0.0 copy-start.9
  49.5 0.0 copy-start.2
  49.5 0.0 copy-start.4
  49.5 0.0 copy-start.5
  49.5 0.0 copy-start.6
  49.5 0.0 copy-start.7
  49.5 6.9 %all-to-all-start.1 = ((bf16[128,32,256]{2,1,0:T(8,128)(2,1)}), bf16[128,32,256]{2,1,0:T(8,128)(2,1)S(1)}, u32[]{:S(2)}, u32[]{:S(2)}) async-start(bf16[128,32,256]{2,1,0:T(8,128)(2,1)} %bitcast.9), calls=%async_computation.1 | async-start | bytes 4194304 | tf_op jit(solution)/shard_map/all_to_all | solution.py:395
  56.4 0.0 copy-done.9
  56.4 0.0 copy-done.2
  56.4 0.2 copy.26
  56.6 29.3 %all-to-all-done.1 = bf16[128,32,256]{2,1,0:T(8,128)(2,1)S(1)} async-done(((bf16[128,32,256]{2,1,0:T(8,128)(2,1)}), bf16[128,32,256]{2,1,0:T(8,128)(2,1)S(1)}, u32[]{:S(2)}, u32[]{:S(2)}) %all-to-all-start.1) | async-done | bytes 2097184 | tf_op jit(solution)/shard_map/all_to_all | solution.py:395
  85.9 0.0 copy-done.4
  85.9 0.0 copy-done.5
  85.9 0.0 copy-done.6
  85.9 0.0 copy-done.7
  85.9 0.0 copy-start.1
  85.9 1.6 copy-done.1
  87.5 49.5 %attention.1 = (bf16[16,256,256]{2,1,0:T(8,128)(2,1)}, bf16[3072,128]{1,0:T(8,128)(2,1)S(1)}) custom-call(s32[16]{0:T(128)S(1)} %copy-done.7, s32[4096]{0:T(1024)S(1)} %bitcast.37, bf16[4096,256]{1,0:T(8,128)(2,1)S(1)} %bitcast.31, bf16[16,256,256]{2,1,0:T(8,128)(2,1)S(1)} %copy-done.1, f32[256,256]{1,0:T(8,128)S(1)} %copy-done.4, f32[1,256]{1,0:T(1,128)S(1)} %bitcast.38, ...), custom_call_target="tpu_custom_call" | custom-call | tf_op jit(solution)/shard_map/attention/pallas_call | solution.py:235
  137.0 21.0 %all_to_all.27.parts_ref = bf16[128,24,128]{2,1,0:T(8,128)(2,1)S(1)} all-to-all(bf16[128,24,128]{2,1,0:T(8,128)(2,1)S(1)} %bitcast.36), channel_id=1, replica_groups=mesh['batch'=8,'item'=16] {'batch','item'}, dimensions={0} | all-to-all | bytes 1572864 | tf_op jit(solution)/shard_map/all_to_all | solution.py:395
  158.0 0.2 sum_spread.1
  158.2 20.4 %all_to_all.28 = bf16[128,24,128]{2,1,0:T(8,128)(2,1)S(1)} all-to-all(bf16[128,24,128]{2,1,0:T(8,128)(2,1)S(1)} %sum_spread.1), channel_id=1, replica_groups=mesh['batch'=8,'item'=16] {'batch','item'}, dimensions={0} | all-to-all | bytes 1572864 | tf_op jit(solution)/shard_map/all_to_all | solution.py:395
  178.6 0.2 bitcast_convert_fusion
  178.7 0.6 slice_bitcast_fusion
  179.4 0.0 copy-start.8
  179.4 0.9 pad_maximum_fusion.3
  180.3 0.2 copy-done.8
  (10 shorter events, 0.1 us)
Async XLA Ops:
  0.6 10.2 %copy-start = (bf16[16,4,128,128]{3,2,1,0:T(8,128)(2,1)S(1)}, bf16[16,4,128,128]{3,2,1,0:T(8,128)(2,1)}, u32[]{:S(2)}) copy-start(bf16[16,4,128,128]{3,2,1,0:T(8,128)(2,1)} %param.12) | copy-start | bytes 6291460
  3.1 7.8 %collective-permute-start.2 = (bf16[4,2,4,128,128]{4,3,2,1,0:T(8,128)(2,1)}, bf16[4,2,4,128,128]{4,3,2,1,0:T(8,128)(2,1)S(1)}, u32[]{:S(2)}, u32[]{:S(2)}) collective-permute-start(bf16[4,2,4,128,128]{4,3,2,1,0:T(8,128)(2,1)} %dynamic-slice_bitcast_fusion), channel_id=1, source_target_pairs={{0,16},{16,0},{32,48},{48,32},{64,80},{80,64},{96,112},{112,96},{1... | collective-permute-start | bytes 3145736 | tf_op jit(solution)/shard_map/ppermute | solution.py:419
  4.5 38.2 %collective-permute-start = (bf16[2048,256]{1,0:T(8,128)(2,1)}, bf16[2048,256]{1,0:T(8,128)(2,1)}, u32[]{:S(2)}, u32[]{:S(2)}) collective-permute-start(bf16[2048,256]{1,0:T(8,128)(2,1)} %own_ref.1), channel_id=1, source_target_pairs={{0,1},{1,2},{2,3},{3,4},{4,5},{5,6},{6,7},{7,8},{8,9},{9,10},{10,1... | collective-permute-start | bytes 3145736 | tf_op jit(solution)/shard_map/ppermute | solution.py:413
  6.3 36.5 %collective-permute-start.1 = (bf16[2048,256]{1,0:T(8,128)(2,1)}, bf16[2048,256]{1,0:T(8,128)(2,1)}, u32[]{:S(2)}, u32[]{:S(2)}) collective-permute-start(bf16[2048,256]{1,0:T(8,128)(2,1)} %own_ref.1), channel_id=1, source_target_pairs={{1,0},{2,1},{3,2},{4,3},{5,4},{6,5},{7,6},{8,7},{9,8},{10,9},{11,1... | collective-permute-start | bytes 3145736 | tf_op jit(solution)/shard_map/ppermute | solution.py:414
  11.0 10.1 %copy-start.10 = (s32[16,4]{0,1:T(4,128)S(1)}, s32[16,4]{0,1:T(4,128)}, u32[]{:S(2)}) copy-start(s32[16,4]{0,1:T(4,128)} %param.11) | copy-start | bytes 772
  11.8 30.9 %collective-permute-start.3 = (bf16[2,2,4,128,128]{4,3,2,1,0:T(8,128)(2,1)}, bf16[2,2,4,128,128]{4,3,2,1,0:T(8,128)(2,1)}, u32[]{:S(2)}, u32[]{:S(2)}) collective-permute-start(bf16[2,2,4,128,128]{4,3,2,1,0:T(8,128)(2,1)} %pad_maximum_fusion), channel_id=1, source_target_pairs={{0,32},{16,48},{32,64},{48,80},{64,96},{80,112},{96,0},{112,16},{1... | collective-permute-start | bytes 1572872 | tf_op jit(solution)/shard_map/ppermute | solution.py:432
  13.9 28.9 %collective-permute-start.4 = (bf16[2,2,4,128,128]{4,3,2,1,0:T(8,128)(2,1)}, bf16[2,2,4,128,128]{4,3,2,1,0:T(8,128)(2,1)}, u32[]{:S(2)}, u32[]{:S(2)}) collective-permute-start(bf16[2,2,4,128,128]{4,3,2,1,0:T(8,128)(2,1)} %pad_maximum_fusion.1), channel_id=1, source_target_pairs={{0,64},{16,80},{32,96},{48,112},{64,0},{80,16},{96,32},{112,48},{1... | collective-permute-start | bytes 1572872 | tf_op jit(solution)/shard_map/ppermute | solution.py:432
  17.1 25.6 %collective-permute-start.5 = (bf16[2,2,4,128,128]{4,3,2,1,0:T(8,128)(2,1)}, bf16[2,2,4,128,128]{4,3,2,1,0:T(8,128)(2,1)}, u32[]{:S(2)}, u32[]{:S(2)}) collective-permute-start(bf16[2,2,4,128,128]{4,3,2,1,0:T(8,128)(2,1)} %pad_maximum_fusion.2), channel_id=1, source_target_pairs={{0,96},{16,112},{32,0},{48,16},{64,32},{80,48},{96,64},{112,80},{1... | collective-permute-start | bytes 1572872 | tf_op jit(solution)/shard_map/ppermute | solution.py:432
  23.1 19.4 %all-to-all-start = ((s32[128,1,40]{2,1,0:T(1,128)}), s32[128,1,40]{2,1,0:T(1,128)S(1)}, u32[]{:S(2)}, u32[]{:S(2)}) async-start(s32[128,1,40]{2,1,0:T(1,128)} %bitcast), calls=%async_computation | async-start | bytes 131072 | tf_op jit(solution)/shard_map/all_to_all | solution.py:395
  42.7 1.2 copy-start.3
  49.5 7.0 %copy-start.9 = (s32[16,256]{1,0:T(8,128)S(1)}, s32[16,256]{1,0:T(8,128)}, u32[]{:S(2)}) copy-start(s32[16,256]{1,0:T(8,128)} %get-tuple-element.9) | copy-start | bytes 49156
  49.5 7.0 %copy-start.2 = (bf16[256,768]{1,0:T(8,128)(2,1)S(1)}, bf16[256,768]{1,0:T(8,128)(2,1)}, u32[]{:S(2)}) copy-start(bf16[256,768]{1,0:T(8,128)(2,1)} %win_ref.1) | copy-start | bytes 1179652
  49.5 36.4 %copy-start.4 = (f32[256,256]{1,0:T(8,128)S(1)}, f32[256,256]{1,0:T(8,128)}, u32[]{:S(2)}) copy-start(f32[256,256]{1,0:T(8,128)} %pos_ref.1) | copy-start | bytes 786436
  49.5 36.4 %copy-start.5 = (bf16[256,256]{1,0:T(8,128)(2,1)S(1)}, bf16[256,256]{1,0:T(8,128)(2,1)}, u32[]{:S(2)}) copy-start(bf16[256,256]{1,0:T(8,128)(2,1)} %wout_ref.1) | copy-start | bytes 393220
  49.5 36.4 %copy-start.6 = (f32[256]{0:T(256)S(1)}, f32[256]{0:T(256)}, u32[]{:S(2)}) copy-start(f32[256]{0:T(256)} %param.16) | copy-start | bytes 3076
  49.5 36.4 %copy-start.7 = (s32[16]{0:T(128)S(1)}, s32[16]{0:T(128)}, u32[]{:S(2)}) copy-start(s32[16]{0:T(128)} %lens_ref.1) | copy-start | bytes 196
  49.5 36.4 %all-to-all-start.1 = ((bf16[128,32,256]{2,1,0:T(8,128)(2,1)}), bf16[128,32,256]{2,1,0:T(8,128)(2,1)S(1)}, u32[]{:S(2)}, u32[]{:S(2)}) async-start(bf16[128,32,256]{2,1,0:T(8,128)(2,1)} %bitcast.9), calls=%async_computation.1 | async-start | bytes 4194304 | tf_op jit(solution)/shard_map/all_to_all | solution.py:395
  85.9 1.6 copy-start.1
  179.4 1.1 copy-start.8

commit v5 on v4

--- a/solution.py
+++ b/solution.py
@@ -135,6 +135,8 @@
     made, soft = {}, {}
     head(0)
     for t in range(len(items) + 2):
+        if 0 <= t - 1 < len(items):
+            soft[t - 1] = soften(*items[t - 1], made.pop(t - 1))
         if t < len(items):
             bring(t, len(items))
             if t == 3:
@@ -144,9 +146,6 @@
             collect(*items[t - 2], soft.pop(t - 2))
         if t - 2 == first - 1 + 2:
             tail(0)
-        s = t - 1
-        if 0 <= s < len(items):
-            soft[s] = soften(*items[s], made.pop(s))
     tail(1)
 
 

time: 181 us -> 173 us (0.956)
  Pallas kernels: 57.8 us -> 44.3 us
  blocking collectives: 41.4 us -> 47.3 us
    pallas_call x1, Pallas kernels: 49.5 us -> 35.9 us  [attention(): pl.pallas_call(attn_kernel, out_shape=(jax.ShapeDtypeStruct((users, lengt...]
    all_to_all x2, blocking collectives: 41.4 us -> 47.3 us  [exchange(): return lax.all_to_all(cells, axes, split_axis=0, concat_axis=0, tiled=True)]
where the time goes in v5:
time: 173 us
  blocking collectives  47.3 us (27%)
  Pallas kernels  44.3 us (26%)
  waiting for transfers between devices  43.7 us (25%)
  starting transfers between devices  24.4 us (14%)
  local copies, waits for them, and re-layouts  8.73 us (5%)
  other arithmetic  3.55 us (2%)
    all_to_all x2, blocking collectives, exchange(): return lax.all_to_all(cells, axes, split_axis=0, concat_axis=0, tiled=True)  47.3 us
    all_to_all x2, waiting for transfers between devices, exchange(): return lax.all_to_all(cells, axes, split_axis=0, concat_axis=0, tiled=True)  43.7 us
    pallas_call x1, Pallas kernels, attention(): pl.pallas_call(attn_kernel, out_shape=(jax.ShapeDtypeStruct((users, lengt...  35.9 us
    all_to_all x2, starting transfers between devices, exchange(): return lax.all_to_all(cells, axes, split_axis=0, concat_axis=0, tiled=True)  11.8 us
    pallas_call x1, Pallas kernels, graph(): pl.pallas_call(graph_kernel, out_shape=jax.ShapeDtypeStruct((count, feat)...  5.47 us
    ppermute x3, starting transfers between devices, local(): lax.ppermute(pair, 'batch', [(i, (i + 2 * k) % n_batch) for i in range(n_...  4.81 us
    ppermute x1, starting transfers between devices, local(): lax.ppermute(item_table, 'item', [((i + 1) % n_item, i) for i in range(n_...  4.57 us
  transfers between devices with their start and end apart: 8, of which 2 were waited for; matrix products, arithmetic and copies ran while one was open for 3% of the time, Pallas kernels for 2%

profile of v5, /device:TPU:1, one launch (start us, length us, event | category | flops | bytes accessed | tf_op | source)
XLA Modules:
  0.0 172.8 jit_solution(15978943543284831152)
XLA Ops:
  0.6 0.0 copy-start
  0.6 2.5 %dynamic-slice_bitcast_fusion = bf16[4,2,4,128,128]{4,3,2,1,0:T(8,128)(2,1)} fusion(bf16[4,2,2,4,128,128]{5,4,3,2,1,0:T(8,128)(2,1)} %bitcast.32, s32[]{:T(128)S(6)} %select_n.38), kind=kLoop, calls=%fused_computation | loop fusion | bytes 2097156 | tf_op jit(solution)/shard_map/jit(dynamic_index_in_dim)/squeeze | solution.py:419
  3.1 1.4 collective-permute-start.2
  4.5 1.7 collective-permute-start
  6.3 4.6 %collective-permute-start.1 = (bf16[2048,256]{1,0:T(8,128)(2,1)}, bf16[2048,256]{1,0:T(8,128)(2,1)}, u32[]{:S(2)}, u32[]{:S(2)}) collective-permute-start(bf16[2048,256]{1,0:T(8,128)(2,1)} %own_ref.1), channel_id=1, source_target_pairs={{1,0},{2,1},{3,2},{4,3},{5,4},{6,5},{7,6},{8,7},{9,8},{10,9},{11,1... | collective-permute-start | bytes 3145736 | tf_op jit(solution)/shard_map/ppermute | solution.py:413
  10.8 0.0 copy-done
  10.8 0.1 dynamic-slice_bitcast_fusion.1
  10.9 0.0 collective-permute-done.2.swapped_ref
  10.9 0.1 constant_dynamic-slice_fusion
  11.0 0.0 copy-start.10
  11.0 0.8 pad_maximum_fusion
  11.8 1.2 collective-permute-start.3
  13.0 0.8 pad_maximum_fusion.1
  13.9 2.5 %collective-permute-start.4 = (bf16[2,2,4,128,128]{4,3,2,1,0:T(8,128)(2,1)}, bf16[2,2,4,128,128]{4,3,2,1,0:T(8,128)(2,1)}, u32[]{:S(2)}, u32[]{:S(2)}) collective-permute-start(bf16[2,2,4,128,128]{4,3,2,1,0:T(8,128)(2,1)} %pad_maximum_fusion.1), channel_id=1, source_target_pairs={{0,64},{16,80},{32,96},{48,112},{64,0},{80,16},{96,32},{112,48},{1... | collective-permute-start | bytes 1572872 | tf_op jit(solution)/shard_map/ppermute | solution.py:431
  16.3 0.8 pad_maximum_fusion.2
  17.1 1.2 collective-permute-start.5
  18.3 2.7 %route.1 = (s32[128,32]{1,0:T(8,128)}, s32[16,256]{1,0:T(8,128)}) custom-call(s32[16,256]{1,0:T(8,128)} %hist_ref.1), custom_call_target="tpu_custom_call" | custom-call | tf_op jit(solution)/shard_map/route/pallas_call | solution.py:295
  21.0 0.0 copy-done.10
  21.0 0.1 copy.21
  21.1 0.1 broadcast_in_dim.7
  21.2 0.1 copy.22
  21.3 0.1 broadcast_in_dim.8
  21.3 0.1 reshape.55
  21.4 0.9 copy.23
  22.3 0.8 copy.24
  23.1 5.0 %all-to-all-start = ((s32[128,1,40]{2,1,0:T(1,128)}), s32[128,1,40]{2,1,0:T(1,128)S(1)}, u32[]{:S(2)}, u32[]{:S(2)}) async-start(s32[128,1,40]{2,1,0:T(1,128)} %bitcast), calls=%async_computation | async-start | bytes 131072 | tf_op jit(solution)/shard_map/all_to_all | solution.py:394
  28.1 14.4 %all-to-all-done = s32[128,1,40]{2,1,0:T(1,128)S(1)} async-done(((s32[128,1,40]{2,1,0:T(1,128)}), s32[128,1,40]{2,1,0:T(1,128)S(1)}, u32[]{:S(2)}, u32[]{:S(2)}) %all-to-all-start) | async-done | bytes 20512 | tf_op jit(solution)/shard_map/all_to_all | solution.py:394
  42.4 0.1 slice.52
  42.5 0.1 reshape.57.tile_ref
  42.6 0.1 reshape.60.refs_3_
  42.7 0.0 collective-permute-done.left_ref
  42.7 0.0 collective-permute-done.1.right_ref
  42.7 0.0 collective-permute-done.3.refs_0_
  42.7 0.0 collective-permute-done.4.refs_1_
  42.7 0.0 collective-permute-done.5.refs_2_
  42.7 0.0 copy-start.3
  42.8 1.2 copy-done.3
  44.0 5.5 %graph.1 = bf16[4096,256]{1,0:T(8,128)(2,1)} custom-call(s32[64]{0:T(128)S(1)} %reshape.57.tile_ref, s32[1]{0:T(128)} %bitcast.3.part_ref, bf16[2048,256]{1,0:T(8,128)(2,1)} %collective-permute-done.left_ref, bf16[2048,256]{1,0:T(8,128)(2,1)S(1)} %copy-done.3, bf16[2048,256]{1,0:T(8,128)(2,1)} %collective-permute-done.1.right_ref, ...), custom_call_target="tpu_custom_call" | custom-call | tf_op jit(solution)/shard_map/graph/pallas_call | solution.py:364
  49.5 0.0 copy-start.9
  49.5 0.0 copy-start.2
  49.5 0.0 copy-start.4
  49.5 0.0 copy-start.5
  49.5 0.0 copy-start.6
  49.5 0.0 copy-start.7
  49.5 6.9 %all-to-all-start.1 = ((bf16[128,32,256]{2,1,0:T(8,128)(2,1)}), bf16[128,32,256]{2,1,0:T(8,128)(2,1)S(1)}, u32[]{:S(2)}, u32[]{:S(2)}) async-start(bf16[128,32,256]{2,1,0:T(8,128)(2,1)} %bitcast.9), calls=%async_computation.1 | async-start | bytes 4194304 | tf_op jit(solution)/shard_map/all_to_all | solution.py:394
  56.4 0.0 copy-done.9
  56.4 0.0 copy-done.2
  56.4 0.2 copy.26
  56.6 29.3 %all-to-all-done.1 = bf16[128,32,256]{2,1,0:T(8,128)(2,1)S(1)} async-done(((bf16[128,32,256]{2,1,0:T(8,128)(2,1)}), bf16[128,32,256]{2,1,0:T(8,128)(2,1)S(1)}, u32[]{:S(2)}, u32[]{:S(2)}) %all-to-all-start.1) | async-done | bytes 2097184 | tf_op jit(solution)/shard_map/all_to_all | solution.py:394
  85.9 0.0 copy-done.4
  85.9 0.0 copy-done.5
  85.9 0.0 copy-done.6
  85.9 0.0 copy-done.7
  85.9 0.0 copy-start.1
  85.9 1.6 copy-done.1
  87.5 35.9 %attention.1 = (bf16[16,256,256]{2,1,0:T(8,128)(2,1)}, bf16[3072,128]{1,0:T(8,128)(2,1)S(1)}) custom-call(s32[16]{0:T(128)S(1)} %copy-done.7, s32[4096]{0:T(1024)S(1)} %bitcast.37, bf16[4096,256]{1,0:T(8,128)(2,1)S(1)} %bitcast.31, bf16[16,256,256]{2,1,0:T(8,128)(2,1)S(1)} %copy-done.1, f32[256,256]{1,0:T(8,128)S(1)} %copy-done.4, f32[1,256]{1,0:T(1,128)S(1)} %bitcast.38, ...), custom_call_target="tpu_custom_call" | custom-call | tf_op jit(solution)/shard_map/attention/pallas_call | solution.py:234
  123.4 27.0 %all_to_all.27.parts_ref = bf16[128,24,128]{2,1,0:T(8,128)(2,1)S(1)} all-to-all(bf16[128,24,128]{2,1,0:T(8,128)(2,1)S(1)} %bitcast.36), channel_id=1, replica_groups=mesh['batch'=8,'item'=16] {'batch','item'}, dimensions={0} | all-to-all | bytes 1572864 | tf_op jit(solution)/shard_map/all_to_all | solution.py:394
  150.4 0.2 sum_spread.1
  150.6 20.4 %all_to_all.28 = bf16[128,24,128]{2,1,0:T(8,128)(2,1)S(1)} all-to-all(bf16[128,24,128]{2,1,0:T(8,128)(2,1)S(1)} %sum_spread.1), channel_id=1, replica_groups=mesh['batch'=8,'item'=16] {'batch','item'}, dimensions={0} | all-to-all | bytes 1572864 | tf_op jit(solution)/shard_map/all_to_all | solution.py:394
  170.9 0.2 bitcast_convert_fusion
  171.1 0.6 slice_bitcast_fusion
  171.8 0.0 copy-start.8
  171.8 0.9 pad_maximum_fusion.3
  172.7 0.2 copy-done.8
  (10 shorter events, 0.1 us)
Async XLA Ops:
  0.6 10.2 %copy-start = (bf16[16,4,128,128]{3,2,1,0:T(8,128)(2,1)S(1)}, bf16[16,4,128,128]{3,2,1,0:T(8,128)(2,1)}, u32[]{:S(2)}) copy-start(bf16[16,4,128,128]{3,2,1,0:T(8,128)(2,1)} %param.12) | copy-start | bytes 6291460
  3.1 7.8 %collective-permute-start.2 = (bf16[4,2,4,128,128]{4,3,2,1,0:T(8,128)(2,1)}, bf16[4,2,4,128,128]{4,3,2,1,0:T(8,128)(2,1)S(1)}, u32[]{:S(2)}, u32[]{:S(2)}) collective-permute-start(bf16[4,2,4,128,128]{4,3,2,1,0:T(8,128)(2,1)} %dynamic-slice_bitcast_fusion), channel_id=1, source_target_pairs={{0,16},{16,0},{32,48},{48,32},{64,80},{80,64},{96,112},{112,96},{1... | collective-permute-start | bytes 3145736 | tf_op jit(solution)/shard_map/ppermute | solution.py:418
  4.5 38.2 %collective-permute-start = (bf16[2048,256]{1,0:T(8,128)(2,1)}, bf16[2048,256]{1,0:T(8,128)(2,1)}, u32[]{:S(2)}, u32[]{:S(2)}) collective-permute-start(bf16[2048,256]{1,0:T(8,128)(2,1)} %own_ref.1), channel_id=1, source_target_pairs={{0,1},{1,2},{2,3},{3,4},{4,5},{5,6},{6,7},{7,8},{8,9},{9,10},{10,1... | collective-permute-start | bytes 3145736 | tf_op jit(solution)/shard_map/ppermute | solution.py:412
  6.3 36.5 %collective-permute-start.1 = (bf16[2048,256]{1,0:T(8,128)(2,1)}, bf16[2048,256]{1,0:T(8,128)(2,1)}, u32[]{:S(2)}, u32[]{:S(2)}) collective-permute-start(bf16[2048,256]{1,0:T(8,128)(2,1)} %own_ref.1), channel_id=1, source_target_pairs={{1,0},{2,1},{3,2},{4,3},{5,4},{6,5},{7,6},{8,7},{9,8},{10,9},{11,1... | collective-permute-start | bytes 3145736 | tf_op jit(solution)/shard_map/ppermute | solution.py:413
  11.0 10.1 %copy-start.10 = (s32[16,4]{0,1:T(4,128)S(1)}, s32[16,4]{0,1:T(4,128)}, u32[]{:S(2)}) copy-start(s32[16,4]{0,1:T(4,128)} %param.11) | copy-start | bytes 772
  11.8 30.9 %collective-permute-start.3 = (bf16[2,2,4,128,128]{4,3,2,1,0:T(8,128)(2,1)}, bf16[2,2,4,128,128]{4,3,2,1,0:T(8,128)(2,1)}, u32[]{:S(2)}, u32[]{:S(2)}) collective-permute-start(bf16[2,2,4,128,128]{4,3,2,1,0:T(8,128)(2,1)} %pad_maximum_fusion), channel_id=1, source_target_pairs={{0,32},{16,48},{32,64},{48,80},{64,96},{80,112},{96,0},{112,16},{1... | collective-permute-start | bytes 1572872 | tf_op jit(solution)/shard_map/ppermute | solution.py:431
  13.9 28.9 %collective-permute-start.4 = (bf16[2,2,4,128,128]{4,3,2,1,0:T(8,128)(2,1)}, bf16[2,2,4,128,128]{4,3,2,1,0:T(8,128)(2,1)}, u32[]{:S(2)}, u32[]{:S(2)}) collective-permute-start(bf16[2,2,4,128,128]{4,3,2,1,0:T(8,128)(2,1)} %pad_maximum_fusion.1), channel_id=1, source_target_pairs={{0,64},{16,80},{32,96},{48,112},{64,0},{80,16},{96,32},{112,48},{1... | collective-permute-start | bytes 1572872 | tf_op jit(solution)/shard_map/ppermute | solution.py:431
  17.1 25.6 %collective-permute-start.5 = (bf16[2,2,4,128,128]{4,3,2,1,0:T(8,128)(2,1)}, bf16[2,2,4,128,128]{4,3,2,1,0:T(8,128)(2,1)}, u32[]{:S(2)}, u32[]{:S(2)}) collective-permute-start(bf16[2,2,4,128,128]{4,3,2,1,0:T(8,128)(2,1)} %pad_maximum_fusion.2), channel_id=1, source_target_pairs={{0,96},{16,112},{32,0},{48,16},{64,32},{80,48},{96,64},{112,80},{1... | collective-permute-start | bytes 1572872 | tf_op jit(solution)/shard_map/ppermute | solution.py:431
  23.1 19.4 %all-to-all-start = ((s32[128,1,40]{2,1,0:T(1,128)}), s32[128,1,40]{2,1,0:T(1,128)S(1)}, u32[]{:S(2)}, u32[]{:S(2)}) async-start(s32[128,1,40]{2,1,0:T(1,128)} %bitcast), calls=%async_computation | async-start | bytes 131072 | tf_op jit(solution)/shard_map/all_to_all | solution.py:394
  42.7 1.2 copy-start.3
  49.5 7.0 %copy-start.9 = (s32[16,256]{1,0:T(8,128)S(1)}, s32[16,256]{1,0:T(8,128)}, u32[]{:S(2)}) copy-start(s32[16,256]{1,0:T(8,128)} %get-tuple-element.9) | copy-start | bytes 49156
  49.5 7.0 %copy-start.2 = (bf16[256,768]{1,0:T(8,128)(2,1)S(1)}, bf16[256,768]{1,0:T(8,128)(2,1)}, u32[]{:S(2)}) copy-start(bf16[256,768]{1,0:T(8,128)(2,1)} %win_ref.1) | copy-start | bytes 1179652
  49.5 36.4 %copy-start.4 = (f32[256,256]{1,0:T(8,128)S(1)}, f32[256,256]{1,0:T(8,128)}, u32[]{:S(2)}) copy-start(f32[256,256]{1,0:T(8,128)} %pos_ref.1) | copy-start | bytes 786436
  49.5 36.4 %copy-start.5 = (bf16[256,256]{1,0:T(8,128)(2,1)S(1)}, bf16[256,256]{1,0:T(8,128)(2,1)}, u32[]{:S(2)}) copy-start(bf16[256,256]{1,0:T(8,128)(2,1)} %wout_ref.1) | copy-start | bytes 393220
  49.5 36.4 %copy-start.6 = (f32[256]{0:T(256)S(1)}, f32[256]{0:T(256)}, u32[]{:S(2)}) copy-start(f32[256]{0:T(256)} %param.16) | copy-start | bytes 3076
  49.5 36.4 %copy-start.7 = (s32[16]{0:T(128)S(1)}, s32[16]{0:T(128)}, u32[]{:S(2)}) copy-start(s32[16]{0:T(128)} %lens_ref.1) | copy-start | bytes 196
  49.5 36.4 %all-to-all-start.1 = ((bf16[128,32,256]{2,1,0:T(8,128)(2,1)}), bf16[128,32,256]{2,1,0:T(8,128)(2,1)S(1)}, u32[]{:S(2)}, u32[]{:S(2)}) async-start(bf16[128,32,256]{2,1,0:T(8,128)(2,1)} %bitcast.9), calls=%async_computation.1 | async-start | bytes 4194304 | tf_op jit(solution)/shard_map/all_to_all | solution.py:394
  85.9 1.6 copy-start.1
  171.8 1.1 copy-start.8
